TPU v7x, 128 devices: a whole 4x4x4 slice. The times are simulated.
128 devices in a mesh: fx: 8 (over y_hi, z), fy: 16 (over x, y_lo, core).
Axes of the slice: x: 4, y: 4 (y_hi: 2, y_lo: 2; y = y_hi * 2 + y_lo), z: 4, core: 2. Of those that a mesh axis runs over, the one named last changes fastest.
Arguments:
- facets: float32 [8192, 4096], P('fx', 'fy'), may hold values from -6 to 6
- counts: int32 [8, 16], P('fx', 'fy'), may hold values from 1 to 16, as said below
- cells: int32 [2, 8, 16, 2048], P(None, 'fx', 'fy'), may hold values from 0 to 248
- fracs: float32 [2, 8, 16, 2048], P(None, 'fx', 'fy'), may hold values from 0 to 1
Outputs:
- predictions: float32 [2, 8, 16, 2048], P(None, 'fx', 'fy')
Inputs may be any that keep to these rules, and one draw needn't show every extreme that they name: Blocks 0 to counts - 1 of a subgrid's 128-visibility blocks are live, the others are padding; some subgrid has 16 live blocks.
All inputs are finite; a program needn't handle non-finite values.
Results may differ from a plain program's by a relative error of at most 0.0003.
Values sent between devices are 32-bit elements; how exact they have to be, the bound alone decides.
A program may use at most 128 MiB of HBM per device.

v0:
```python
import math

import jax
import jax.numpy as jnp
from jax import lax
from jax.sharding import Mesh
from jax.sharding import PartitionSpec as P

NIMG = 65536
FP = 4096
SUBGRID = 256
SUPPORT = 8
VBLOCK = 128
FX = ("fx_0", "fx_1")


def sum_in_order(blocks, axes, turns):
    dims = [lax.axis_size(a) for a in axes]
    blocks = blocks.reshape(*dims, *blocks.shape[1:])
    blocks = blocks.transpose(*turns, *range(len(axes), blocks.ndim))
    blocks = blocks.reshape(-1, *blocks.shape[len(axes) :])
    for k in turns:
        blocks = lax.psum_scatter(blocks, axes[k], scatter_dimension=0, tiled=True)
    return blocks[0]


def split_up(array, dim, length):
    before, after = (array.shape[:dim], array.shape[dim + 1 :])
    return jnp.moveaxis(array.reshape(*before, length, -1, *after), dim, 0)


def summed_rows(array, axes, turns, dim):
    length = lax.axis_size(axes)
    return sum_in_order(split_up(array, dim, length), axes, turns)


def mulmod(upper, lower):
    low = upper % 256
    high = upper // 256
    return (low * lower + 256 * (high * lower % (NIMG // 256))) % NIMG


def factor(freqs, pixels, scale):
    inner = pixels % FP
    turns = mulmod(freqs[:, None], pixels[None, :])
    angle = turns.astype(jnp.float32) * (2.0 * math.pi / NIMG)
    window = jnp.sin(math.pi * (inner.astype(jnp.float32) + 0.5) / FP) * scale
    return (jnp.cos(angle) * window[None, :], -jnp.sin(angle) * window[None, :])


def kernel(offset, frac):
    positions = jnp.arange(SUBGRID, dtype=jnp.int32)
    dist = positions[None, :] - offset[:, None]
    inside = (dist >= 0) & (dist < SUPPORT)
    shift = dist.astype(jnp.float32) - (SUPPORT // 2 - 1) - frac[:, None]
    value = 0.6 * jnp.exp(-shift * shift / 4.5)
    return jnp.where(inside, value, jnp.zeros_like(value))


def column_term(v_start, v_count, p_real, p_imag, columns, scale):
    freqs = v_start * SUBGRID + jnp.arange(v_count * SUBGRID, dtype=jnp.int32)
    b_real, b_imag = factor(freqs, columns, scale)
    left = jnp.concatenate([b_real, b_imag], axis=0)
    right = jnp.concatenate([p_real, p_imag], axis=0)
    product = lax.dot_general(
        left,
        right,
        (((1,), (1,)), ((), ())),
        precision=lax.Precision.HIGHEST,
        preferred_element_type=jnp.float32,
    )
    height = v_count * SUBGRID
    width = p_real.shape[0]
    t_real = product[:height, :width] - product[height:, width:]
    t_imag = product[height:, :width] + product[:height, width:]
    return jnp.stack(
        [t_real.reshape(v_count, SUBGRID, width), t_imag.reshape(v_count, SUBGRID, width)], axis=1
    )


def degrid(values, grid, cell_rows, frac_rows, row, col, stride, turns):
    highest = lax.Precision.HIGHEST

    def step(turn, values):
        offset = stride * turn * VBLOCK
        cells_u = lax.dynamic_slice_in_dim(cell_rows[0], offset, VBLOCK)
        cells_v = lax.dynamic_slice_in_dim(cell_rows[1], offset, VBLOCK)
        fracs_u = lax.dynamic_slice_in_dim(frac_rows[0], offset, VBLOCK)
        fracs_v = lax.dynamic_slice_in_dim(frac_rows[1], offset, VBLOCK)
        weight_u = kernel(cells_u, fracs_u)
        weight_v = kernel(cells_v, fracs_v)
        g_real = jnp.dot(weight_v, grid[0], precision=highest, preferred_element_type=jnp.float32)
        g_imag = jnp.dot(weight_v, grid[1], precision=highest, preferred_element_type=jnp.float32)
        block = jnp.stack([jnp.sum(g_real * weight_u, axis=1), jnp.sum(g_imag * weight_u, axis=1)])
        zero = jnp.zeros((), jnp.int32)
        return lax.dynamic_update_slice(
            values, block[:, None, None, :], (zero, jnp.int32(row), jnp.int32(col), offset)
        )

    return lax.fori_loop(jnp.int32(0), turns, step, values)


def per_device(facets, counts, cells, fracs):
    highest = lax.Precision.HIGHEST
    su_dev = counts.shape[0]
    sv_dev = counts.shape[1]
    local_rows = facets.shape[0]
    local_cols = facets.shape[1]
    row_scale = math.sqrt(2.0 / (local_rows * lax.axis_size(FX)))
    col_scale = math.sqrt(2.0 / (local_cols * lax.axis_size("fy")))
    row_index = lax.axis_index(FX)
    col_index = lax.axis_index("fy")
    my_rows = row_index * local_rows + jnp.arange(local_rows, dtype=jnp.int32)
    count = su_dev * lax.axis_size(FX)
    freqs = jnp.arange(count * SUBGRID, dtype=jnp.int32)
    real_part, imag_part = factor(freqs, my_rows, row_scale)
    table = jnp.stack(
        [
            real_part.reshape(count, SUBGRID, local_rows),
            imag_part.reshape(count, SUBGRID, local_rows),
        ],
        axis=1,
    )
    product = jnp.dot(
        table.reshape(count * 2 * SUBGRID, local_rows),
        facets,
        precision=highest,
        preferred_element_type=jnp.float32,
    )
    partial_sums = summed_rows(product.reshape(count, 2, SUBGRID, local_cols), FX, (1, 0), 0)
    piece = lax.all_gather(partial_sums, "fy", axis=3, tiled=True)
    width = piece.shape[3]
    columns = jnp.arange(width, dtype=jnp.int32)
    term = column_term(
        col_index * sv_dev,
        sv_dev,
        piece[:, 0].reshape(su_dev * SUBGRID, width),
        piece[:, 1].reshape(su_dev * SUBGRID, width),
        columns,
        col_scale,
    )
    blank = jnp.zeros((2, su_dev, sv_dev, cells.shape[3]), jnp.float32)
    values = blank
    grid = term[0, :, :, 0:SUBGRID]
    values = degrid(values, grid, cells[:, 0, 0], fracs[:, 0, 0], 0, 0, 1, counts[0, 0])
    return values


def solution(mesh):
    torus = Mesh(mesh.devices.reshape(2, 4, mesh.shape["fy"]), ("fx_0", "fx_1", "fy"))
    in_specs = (P(FX, "fy"), P(FX, "fy"), P(None, FX, "fy", None), P(None, FX, "fy", None))
    out_specs = P(None, FX, "fy", None)
    return jax.shard_map(
        per_device, mesh=torus, in_specs=in_specs, out_specs=out_specs, check_vma=False
    )
```

profile of v0, /device:TPU:11, one launch (start us, length us, event | category | flops | bytes accessed | tf_op | source)
XLA Modules:
  0.0 242.6 jit_solution(14438846253240212937)
XLA Ops:
  6.5 0.0 copy-start
  6.5 0.0 reduce-scatter.3.cloned.1.call-start
  6.5 0.1 fusion.104
  6.6 0.1 add_select_fusion.6
  6.7 37.7 %cosine_multiply_fusion = (f32[2,4,1,256,1024]{4,3,2,1,0:T(8,128)S(1)}, f32[2,4,1,256,1024]{4,3,2,1,0:T(8,128)S(1)}) fusion(f32[1024]{0:T(1024)S(1)} %fusion.104, s32[2,4,256]{2,1,0:T(4,128)S(1)} %get-tuple-element.134, s32[1024]{0:T(1024)S(1)} %iota_add_fusion.1, s32[2,4,256]{2,1,0:T(4,128)S(1)} %get-tuple-element.133), kind=kLoop, calls=%fused_computation.90 | loop fusion | flops 65011712 | bytes 16801792 | tf_op jit(solution)/shard_map/mul | solution.py:48
  44.4 0.0 copy-done
  44.4 14.9 %fusion.80 = f32[4,2,1,2,256,256]{5,4,3,0,1,2:T(8,128)S(1)} fusion(f32[2,4,1,256,1024]{4,3,2,1,0:T(8,128)S(1)} %get-tuple-element.130, f32[2,4,1,256,1024]{4,3,2,1,0:T(8,128)S(1)} %get-tuple-element.129, f32[1024,256]{1,0:T(8,128)S(1)} %copy-done), kind=kOutput, calls=%fused_computation.110 | convolution fusion | flops 12889096192 | bytes 22020096 | tf_op jit(solution)/shard_map/dot_general | solution.py:124
  59.4 2.4 copy.6
  61.7 0.0 copy-start.3
  61.7 0.0 copy-start.4
  61.7 0.0 reduce-scatter.3.cloned.1.call-update
  61.8 0.0 reduce-scatter.5.cloned.1.call-start
  61.8 49.4 %reduce-scatter.3.cloned.1.call-done = f32[2,1,2,256,256]{4,3,2,0,1:T(8,128)} async-done(((f32[8,1,2,256,256]{4,3,2,0,1:T(8,128)}), f32[2,1,2,256,256]{4,3,2,0,1:T(8,128)}) %reduce-scatter.3.cloned.1.call-update) | async-done | bytes 1048592 | tf_op jit(solution)/shard_map/reduce_scatter | solution.py:23
  111.2 0.0 reduce-scatter.5.cloned.1.call-update
  111.2 0.0 all-gather.3.cloned.1.call-start
  111.3 25.3 %reduce-scatter.5.cloned.1.call-done = f32[1,1,2,256,256]{4,3,2,0,1:T(8,128)} async-done(((f32[2,1,2,256,256]{4,3,2,0,1:T(8,128)}), f32[1,1,2,256,256]{4,3,2,0,1:T(8,128)}) %reduce-scatter.5.cloned.1.call-update) | async-done | bytes 524304 | tf_op jit(solution)/shard_map/reduce_scatter | solution.py:23
  136.6 0.0 all-gather.3.cloned.1.call-update
  136.6 0.0 copy-done.3
  136.6 0.0 copy-done.4
  136.7 0.1 fusion.90
  136.8 20.3 %cosine_multiply_fusion.1 = (f32[256,4096]{1,0:T(8,128)}, f32[256,4096]{1,0:T(8,128)}) fusion(f32[4096]{0:T(1024)S(1)} %fusion.90, s32[256]{0:T(256)S(1)} %get-tuple-element.135, s32[256]{0:T(256)S(1)} %get-tuple-element.136), kind=kLoop, calls=%fused_computation.106 | loop fusion | flops 32505856 | bytes 8407040 | tf_op jit(solution)/shard_map/mul | solution.py:48
  157.1 34.1 %all-gather.3.cloned.1.call-done = f32[1,1,2,256,4096]{4,3,2,0,1:T(8,128)} async-done(((f32[1,1,2,256,256]{4,3,2,0,1:T(8,128)}), f32[1,1,2,256,4096]{4,3,2,0,1:T(8,128)}) %all-gather.3.cloned.1.call-update) | async-done | bytes 8388624 | tf_op jit(solution)/shard_map/all_gather | solution.py:131
  191.2 0.0 copy-start.1
  191.2 0.0 copy-start.2
  191.2 4.1 %slice_bitcast_fusion.1 = (f32[256,4096]{1,0:T(8,128)S(1)}, f32[256,4096]{1,0:T(8,128)S(1)}) fusion(f32[1,2,256,4096]{3,2,1,0:T(8,128)} %bitcast.62), kind=kLoop, calls=%fused_computation.104 | loop fusion | bytes 16777216 | tf_op jit(solution)/shard_map/reshape;squeeze | solution.py:137
  195.3 0.5 copy-done.1
  195.8 1.3 copy-done.2
  197.1 14.3 %fusion.64 = f32[512,512]{1,0:T(8,128)S(1)} fusion(f32[256,4096]{1,0:T(8,128)S(1)} %copy-done.2, f32[256,4096]{1,0:T(8,128)S(1)} %copy-done.1, f32[256,4096]{1,0:T(8,128)S(1)} %get-tuple-element.126, f32[256,4096]{1,0:T(8,128)S(1)} %get-tuple-element.125), kind=kOutput, calls=%fused_computation.82 | convolution fusion | flops 12889096192 | bytes 17825792 | tf_op jit(solution)/shard_map/dot_general | solution.py:65
  211.4 0.1 fusion.85
  211.6 23.9 %while.13 = (s32[]{:T(128)}, f32[2,1,1,2048]{3,2,1,0:T(1,128)S(1)}, s32[]{:T(128)}, s32[2,2048]{1,0:T(2,128)S(1)}, f32[2,2048]{1,0:T(2,128)S(1)}, /*index=5*/f32...) while((s32[]{:T(128)}, f32[2,1,1,2048]{3,2,1,0:T(1,128)S(1)}, s32[]{:T(128)}, ...), condition=%wide.region_5.6_spmd, body=%wide.region_2.5_spmd.sunk | while | flops 203030528 | bytes 603295 | solution.py:100
  212.3 0.4 fusion.129
  212.8 0.4 fusion.128
  214.0 0.4 fusion.129
  214.4 0.4 fusion.128
  215.6 0.4 fusion.129
  216.1 0.4 fusion.128
  217.3 0.4 fusion.129
  217.7 0.4 fusion.128
  219.0 0.4 fusion.129
  219.4 0.4 fusion.128
  220.6 0.4 fusion.129
  221.0 0.4 fusion.128
  222.3 0.4 fusion.129
  222.7 0.4 fusion.128
  223.9 0.4 fusion.129
  224.4 0.4 fusion.128
  225.6 0.4 fusion.129
  226.0 0.4 fusion.128
  227.2 0.4 fusion.129
  227.7 0.4 fusion.128
  228.9 0.4 fusion.129
  229.3 0.4 fusion.128
  230.6 0.4 fusion.129
  231.0 0.4 fusion.128
  232.2 0.4 fusion.129
  232.7 0.4 fusion.128
  233.9 0.4 fusion.129
  234.3 0.4 fusion.128
  235.4 0.0 copy-start.5
  235.5 0.6 copy-done.5
  (91 shorter events, 1.2 us)
Async XLA Ops:
  6.5 37.9 %copy-start = (f32[1024,256]{1,0:T(8,128)S(1)}, f32[1024,256]{1,0:T(8,128)}, u32[]{:S(2)}) copy-start(f32[1024,256]{1,0:T(8,128)} %param.6) | copy-start | bytes 3145732
  6.5 104.7 %reduce-scatter.3.cloned.1.call-start = ((), (), s32[]{:S(2)}) async-start(), calls=%async_computation.2 | async-start | bytes 5242880 | tf_op jit(solution)/shard_map/reduce_scatter | solution.py:23
  61.7 74.9 %copy-start.3 = (f32[2,1,1,2048]{3,2,1,0:T(1,128)S(1)}, f32[2,1,1,2048]{3,2,1,0:T(1,128)}, u32[]{:S(2)}) copy-start(f32[2,1,1,2048]{3,2,1,0:T(1,128)} %param.9) | copy-start | bytes 49156
  61.7 74.9 %copy-start.4 = (s32[2,1,1,2048]{3,2,1,0:T(1,128)S(1)}, s32[2,1,1,2048]{3,2,1,0:T(1,128)}, u32[]{:S(2)}) copy-start(s32[2,1,1,2048]{3,2,1,0:T(1,128)} %param.8) | copy-start | bytes 49156
  61.8 74.8 %reduce-scatter.5.cloned.1.call-start = ((), (), s32[]{:S(2)}) async-start(), calls=%async_computation.3 | async-start | bytes 1572864 | tf_op jit(solution)/shard_map/reduce_scatter | solution.py:23
  111.2 80.0 %all-gather.3.cloned.1.call-start = ((), (), s32[]{:S(2)}) async-start(), calls=%async_computation.4 | async-start | bytes 8912896 | tf_op jit(solution)/shard_map/all_gather | solution.py:131
  191.2 4.6 %copy-start.1 = (f32[256,4096]{1,0:T(8,128)S(1)}, f32[256,4096]{1,0:T(8,128)}, u32[]{:S(2)}) copy-start(f32[256,4096]{1,0:T(8,128)} %get-tuple-element.131) | copy-start | bytes 12582916
  191.2 5.9 %copy-start.2 = (f32[256,4096]{1,0:T(8,128)S(1)}, f32[256,4096]{1,0:T(8,128)}, u32[]{:S(2)}) copy-start(f32[256,4096]{1,0:T(8,128)} %get-tuple-element.132) | copy-start | bytes 12582916
  235.4 0.6 copy-start.5
Sparse Core Ops, SparseCore 0:
  61.9 49.2 reduce-scatter.2
  113.5 22.9 reduce-scatter.4
  138.3 52.8 all-gather.2
where the time goes:
time: 245 us; the launch traced here: 243 us
  waiting for transfers between devices  109 us (44%)
  other arithmetic  58.5 us (24%)
  matrix products  41.5 us (17%)
  between operations  13.2 us (5%)
  loops' own time  10.5 us (4%)
  local copies, waits for them, and re-layouts  9.84 us (4%)
    reduce_scatter x2, waiting for transfers between devices, sum_in_order(): blocks = lax.psum_scatter(blocks, axes[k], scatter_dimension=0, tiled=True)  74.7 us
    mul x2, other arithmetic, factor(): return (jnp.cos(angle) * window[None, :], -jnp.sin(angle) * window[None, :])  58 us
    all_gather x1, waiting for transfers between devices, per_device(): piece = lax.all_gather(partial_sums, 'fy', axis=3, tiled=True)  34.1 us
    dot_general x1, matrix products, per_device(): jnp.dot(table.reshape(count * 2 * SUBGRID, local_rows), facets, precision...  14.9 us
    dot_general x1, matrix products, column_term(): lax.dot_general(left, right, (((1,), (1,)), ((), ())), precision=lax.Prec...  14.3 us
    another operation x1, loops' own time, degrid(): return lax.fori_loop(jnp.int32(0), turns, step, values)  10.5 us
    dot_general x14, matrix products, step(): jnp.dot(weight_v, grid[1], precision=highest, preferred_element_type=jnp....  6.17 us
    dot_general x14, matrix products, step(): jnp.dot(weight_v, grid[0], precision=highest, preferred_element_type=jnp....  6.11 us
  transfers between devices with their start and end apart: 3, of which 3 were waited for; matrix products, arithmetic and copies ran while one was open for 8% of the time, Pallas kernels for 0%

commit v1 on v0

v1 whole, which is shorter than its diff:
```python
import functools
import math

import jax
import jax.numpy as jnp
import numpy as np
from jax import lax
from jax.experimental import pallas as pl
from jax.experimental.pallas import tpu as pltpu
from jax.sharding import PartitionSpec as P

NIMG = 65536
FP = 4096
SUB = 256
SUPPORT = 8
VBLOCK = 128
MESH = pl.DeviceIdType.MESH
BF = jnp.bfloat16
F32 = jnp.float32


def separable(cells, pixels, rank):
    a = np.arange(cells) - (cells - 1) / 2
    b = np.arange(pixels) - (pixels - 1) / 2
    theta = 2 * np.pi * np.outer(a, b) / NIMG
    half = rank // 2
    uc, sc, vc = np.linalg.svd(np.cos(theta), full_matrices=False)
    us, ss, vs = np.linalg.svd(np.sin(theta), full_matrices=False)
    left = np.concatenate([uc[:, :half] * sc[:half], -1j * us[:, :half] * ss[:half]], axis=1)
    right = np.concatenate([vc[:half], vs[:half]], axis=0)
    norm = math.sqrt(pixels)
    return left / norm, right * norm


def axis_tables(parts, pixels, subs, rank):
    left, right = separable(SUB, pixels, rank)
    right = right * math.sqrt(2.0 / (parts * pixels))
    xx = np.arange(pixels)
    mid = SUB * np.arange(subs) + (SUB - 1) / 2
    phase = 2 * np.pi * ((mid[:, None] * xx[None, :]) / NIMG)
    turn = np.concatenate([np.cos(phase), -np.sin(phase)], axis=0)
    x = np.arange(parts * pixels)
    window = np.sin(np.pi * ((x % FP) + 0.5) / FP).reshape(parts, pixels)
    kk = np.arange(SUB)
    at = (kk[:, None] * np.arange(parts)[None, :] * pixels % NIMG) / NIMG
    at = at + ((kk - (SUB - 1) / 2) * ((pixels - 1) / 2) / NIMG)[:, None]
    back = np.exp(-2j * np.pi * at)[:, :, None] * left[:, None, :]
    return turn, right, window, back.reshape(SUB, parts * rank)


def split(x):
    high = x.astype(BF)
    return high, (x - high.astype(F32)).astype(BF)


def mm(a, b, dims):
    return lax.dot_general(a, b, (dims, ((), ())), preferred_element_type=F32)


def mm3(a, b, dims):
    (ah, al), (bh, bl) = a, b
    return mm(ah, bh, dims) + (mm(ah, bl, dims) + mm(al, bh, dims))


NN = ((1,), (0,))
NT = ((1,), (1,))


def weights(offset, frac, shape):
    cell = lax.broadcasted_iota(jnp.int32, shape, 0).astype(F32)
    shift = cell - (offset.astype(F32) + (SUPPORT // 2 - 1))
    inside = jnp.abs(shift - 0.5) < SUPPORT // 2
    shift = shift - frac
    value = 0.6 * jnp.exp(shift * shift * (-1.0 / 4.5))
    return jnp.where(inside, value, 0.0)


def kernel(
    nx, ny, rp, rq, tx_hbm, ty_hbm, back_hbm, f_hbm, counts_hbm, cells_hbm, fracs_hbm, out_ref,
    tx, ty, back, f, counts, cells, fracs, m2, z, r1, t, r2, wv, wu,
    fsem, lsem, s1, v1, s2, v2,
):
    me_x = lax.axis_index("fx")
    me_y = lax.axis_index("fy")
    rows = f.shape[0]
    cols = f.shape[1]
    step = rows // 4

    small = [
        pltpu.make_async_copy(src, dst, lsem.at[i])
        for i, (src, dst) in enumerate(
            [
                (tx_hbm, tx), (ty_hbm, ty), (cells_hbm, cells), (fracs_hbm, fracs),
                (counts_hbm, counts), (back_hbm, back),
            ]
        )
    ]
    big = [
        pltpu.make_async_copy(
            f_hbm.at[pl.ds(i * step, step)], f.at[pl.ds(i * step, step)], fsem.at[i]
        )
        for i in range(4)
    ]
    small[0].start()
    big[0].start()
    small[1].start()
    for copy in big[1:] + small[2:]:
        copy.start()

    barrier = pltpu.get_barrier_semaphore()
    for d in range(1, nx):
        pl.semaphore_signal(
            barrier, inc=1, device_id=(lax.rem(me_x + d, nx), me_y), device_id_type=MESH
        )
    for d in range(1, ny):
        pl.semaphore_signal(
            barrier, inc=1, device_id=(me_x, lax.rem(me_y + d, ny)), device_id_type=MESH
        )

    small[0].wait()
    wx = tx[pl.ds(2 * nx + rp + me_x, 1), :]
    phi = tx[pl.ds(2 * nx, rp), :] * wx
    c1 = None
    for i in range(4):
        lanes = slice(i * step, (i + 1) * step)
        part = jnp.concatenate(
            [
                jnp.broadcast_to(tx[pl.ds(r, 1), lanes], (rp, step)) * phi[:, lanes]
                for r in range(2 * nx)
            ],
            axis=0,
        )
        big[i].wait()
        prod = mm3(split(part), split(f[pl.ds(i * step, step), :]), NN)
        c1 = prod if c1 is None else c1 + prod

    small[1].wait()
    wy = ty[pl.ds(2 * ny + rq + me_y, 1), :]
    phi = ty[pl.ds(2 * ny, rq), :] * wy
    for r in range(2 * ny):
        m2[pl.ds(r * rq, rq), :] = jnp.broadcast_to(ty[pl.ds(r, 1), :], (rq, cols)) * phi
    prod = mm3(split(c1), split(m2[...]), NT)
    hx = nx * rp
    hy = ny * rq
    z[0] = (prod[:hx, :hy] - prod[hx:, hy:]).reshape(nx, rp, hy)
    z[1] = (prod[:hx, hy:] + prod[hx:, :hy]).reshape(nx, rp, hy)

    pl.semaphore_wait(barrier, nx + ny - 2)
    first = []
    for d in range(1, nx):
        peer = lax.rem(me_x + d, nx)
        copy = pltpu.make_async_remote_copy(
            src_ref=z.at[:, peer], dst_ref=r1.at[:, me_x], send_sem=s1.at[d], recv_sem=v1.at[d],
            device_id=(peer, me_y), device_id_type=MESH,
        )
        copy.start()
        first.append(copy)
    r1[:, pl.ds(me_x, 1)] = z[:, pl.ds(me_x, 1)]

    for copy in small[2:5]:
        copy.wait()
    nvis = cells.shape[3]
    wide = 256
    chunks = nvis // wide

    def fill_v(j, carry):
        at = pl.ds(pl.multiple_of(j * wide, wide), wide)
        high, low = split(weights(cells[1, 0, :, at], fracs[1, 0, :, at], (SUB, wide)))
        wv[0, :, at] = high
        wv[1, :, at] = low
        return carry

    lax.fori_loop(0, chunks, fill_v, 0)

    for copy in first:
        copy.wait()
    for c in range(2):
        t[:, :, c * hx : (c + 1) * hx] = r1[c].reshape(hx, hy).T.reshape(ny, rq, hx)
    second = []
    for d in range(1, ny):
        peer = lax.rem(me_y + d, ny)
        copy = pltpu.make_async_remote_copy(
            src_ref=t.at[peer], dst_ref=r2.at[me_y], send_sem=s2.at[d], recv_sem=v2.at[d],
            device_id=(me_x, peer), device_id_type=MESH,
        )
        copy.start()
        second.append(copy)
    r2[pl.ds(me_y, 1)] = t[pl.ds(me_y, 1)]

    def fill_u(j, carry):
        at = pl.ds(pl.multiple_of(j * wide, wide), wide)
        wu[:, at] = weights(cells[0, 0, :, at], fracs[0, 0, :, at], (SUB, wide))
        return carry

    lax.fori_loop(0, chunks, fill_u, 0)
    small[5].wait()

    for copy in second:
        copy.wait()
    got = r2[...].reshape(hy, 2 * hx)
    g_re = got[:, :hx]
    g_im = got[:, hx:]
    g2 = jnp.concatenate(
        [jnp.concatenate([g_re, g_im], axis=1), jnp.concatenate([-g_im, g_re], axis=1)], axis=0
    )
    kx = 2 * hx
    ky = 2 * hy
    vt = (back[2 * SUB : 3 * SUB, :ky], back[2 * SUB : 3 * SUB, ky : 2 * ky])
    ut = (back[: 2 * SUB, :kx], back[: 2 * SUB, kx : 2 * kx])
    half = mm3(vt, split(g2), NN)
    gh, gl = split(mm3(ut, split(half), NT))
    live = counts[...]

    def degrid(j, carry):
        at = pl.ds(pl.multiple_of(j * wide, wide), wide)
        wh = wv[0, :, at]
        wl = wv[1, :, at]
        sums = mm3((gh, gl), (wh, wl), NN)
        w = wu[:, at]
        block = (lax.broadcasted_iota(jnp.int32, (1, wide), 1) + j * wide) // VBLOCK
        alive = block < live
        re = jnp.sum(sums[:SUB] * w, axis=0, keepdims=True)
        im = jnp.sum(sums[SUB:] * w, axis=0, keepdims=True)
        out_ref[0, 0, :, at] = jnp.where(alive, re, 0.0)
        out_ref[1, 0, :, at] = jnp.where(alive, im, 0.0)
        return carry

    lax.fori_loop(0, chunks, degrid, 0)


def solution(mesh):
    nx = mesh.shape["fx"]
    ny = mesh.shape["fy"]
    rp, rq = 16, 8

    def per_device(facets, counts, cells, fracs):
        rows, cols = facets.shape
        nvis = cells.shape[3]
        turn_x, right_x, win_x, back_x = axis_tables(nx, rows, nx, rp)
        turn_y, right_y, win_y, back_y = axis_tables(ny, cols, ny, rq)
        tx = jnp.asarray(np.concatenate([turn_x, right_x, win_x]), F32)
        ty = jnp.asarray(np.concatenate([turn_y, right_y, win_y]), F32)
        back = np.concatenate(
            [
                np.concatenate([back_x.real, -back_x.imag], axis=1),
                np.concatenate([back_x.imag, back_x.real], axis=1),
                np.concatenate([back_y.real, back_y.imag], axis=1),
            ]
        ).astype(np.float32)
        high = back.astype(BF)
        low = (back - high.astype(np.float32)).astype(BF)
        back = jnp.asarray(np.concatenate([high, low], axis=1))
        hx, hy = nx * rp, ny * rq
        any_spec = pl.BlockSpec(memory_space=pltpu.HBM)
        dma = pltpu.SemaphoreType.DMA
        return pl.pallas_call(
            functools.partial(kernel, nx, ny, rp, rq),
            out_shape=jax.ShapeDtypeStruct((2, 1, 1, nvis), F32),
            in_specs=[any_spec] * 7,
            out_specs=pl.BlockSpec(memory_space=pltpu.VMEM),
            scratch_shapes=[
                pltpu.VMEM(tx.shape, F32),
                pltpu.VMEM(ty.shape, F32),
                pltpu.VMEM(back.shape, BF),
                pltpu.VMEM((rows, cols), F32),
                pltpu.VMEM((1, 1), jnp.int32),
                pltpu.VMEM(cells.shape, jnp.int32),
                pltpu.VMEM(fracs.shape, F32),
                pltpu.VMEM((2 * hy, cols), F32),
                pltpu.VMEM((2, nx, rp, hy), F32),
                pltpu.VMEM((2, nx, rp, hy), F32),
                pltpu.VMEM((ny, rq, 2 * hx), F32),
                pltpu.VMEM((ny, rq, 2 * hx), F32),
                pltpu.VMEM((2, SUB, nvis), BF),
                pltpu.VMEM((SUB, nvis), F32),
                dma((4,)),
                dma((6,)),
                dma((nx,)),
                dma((nx,)),
                dma((ny,)),
                dma((ny,)),
            ],
            compiler_params=pltpu.CompilerParams(
                collective_id=0, has_side_effects=True, vmem_limit_bytes=48 << 20
            ),
        )(tx, ty, back, facets, counts, cells, fracs)

    spec = P(None, "fx", "fy", None)
    return jax.shard_map(
        per_device,
        mesh=mesh,
        in_specs=(P("fx", "fy"), P("fx", "fy"), spec, spec),
        out_specs=spec,
        check_vma=False,
    )
```

time: 245 us -> 29 us (0.12)
  the two profiles are of different devices: /device:TPU:11 before, /device:TPU:1 now
where the time goes in v1:
time: 29 us; the launch traced here: 28.7 us
  Pallas kernels  21.9 us (76%)
  local copies, waits for them, and re-layouts  6.13 us (21%)
  between operations  0.67 us (2%)
    pallas_call x1, Pallas kernels, per_device(): pl.pallas_call(functools.partial(kernel, nx, ny, rp, rq), out_shape=jax.S...  21.9 us
    unnamed x13, local copies, waits for them, and re-layouts  6.13 us

profile of v1, /device:TPU:1, one launch (start us, length us, event | category | flops | bytes accessed | tf_op | source)
XLA Modules:
  0.0 28.7 jit_solution(2484147584818652200)
XLA Ops:
  0.7 0.0 copy-start
  0.7 1.2 %copy-done = f32[1024,256]{1,0:T(8,128)S(1)} copy-done((f32[1024,256]{1,0:T(8,128)S(1)}, f32[1024,256]{1,0:T(8,128)}, u32[]{:S(2)}) %copy-start) | copy-done | bytes 1048600
  1.9 0.0 copy-start.1
  1.9 1.1 %copy-done.1 = bf16[768,512]{1,0:T(8,128)(2,1)S(1)} copy-done((bf16[768,512]{1,0:T(8,128)(2,1)S(1)}, bf16[768,512]{1,0:T(8,128)(2,1)}, u32[]{:S(2)}) %copy-start.1) | copy-done | bytes 786456
  3.0 0.0 copy-start.2
  3.0 0.9 %copy-done.2 = f32[40,1024]{1,0:T(8,128)S(1)} copy-done((f32[40,1024]{1,0:T(8,128)S(1)}, f32[40,1024]{1,0:T(8,128)}, u32[]{:S(2)}) %copy-start.2) | copy-done | bytes 163864
  3.9 0.0 copy-start.3
  3.9 0.8 %copy-done.3 = f32[56,256]{1,0:T(8,128)S(1)} copy-done((f32[56,256]{1,0:T(8,128)S(1)}, f32[56,256]{1,0:T(8,128)}, u32[]{:S(2)}) %copy-start.3) | copy-done | bytes 57368
  4.7 0.0 copy-start.4
  4.7 0.7 %copy-done.4 = s32[2,1,1,2048]{3,2,1,0:T(1,128)S(1)} copy-done((s32[2,1,1,2048]{3,2,1,0:T(1,128)S(1)}, s32[2,1,1,2048]{3,2,1,0:T(1,128)}, u32[]{:S(2)}) %copy-start.4) | copy-done | bytes 16408
  5.5 0.0 copy-start.5
  5.5 0.7 %copy-done.5 = f32[2,1,1,2048]{3,2,1,0:T(1,128)S(1)} copy-done((f32[2,1,1,2048]{3,2,1,0:T(1,128)S(1)}, f32[2,1,1,2048]{3,2,1,0:T(1,128)}, u32[]{:S(2)}) %copy-start.5) | copy-done | bytes 16408
  6.2 21.9 %shard_map.73 = f32[2,1,1,2048]{3,2,1,0:T(1,128)S(1)} custom-call(f32[40,1024]{1,0:T(8,128)S(1)} %copy-done.2, f32[56,256]{1,0:T(8,128)S(1)} %copy-done.3, bf16[768,512]{1,0:T(8,128)(2,1)S(1)} %copy-done.1, f32[1024,256]{1,0:T(8,128)S(1)} %copy-done, s32[1,1]{1,0:T(1,128)S(6)} %copy.9.counts_hbm, s32[2,1,1,2048]{3,2,1,0:T(1,128)S(1)} %copy-done.4, ...), custom_call_target="tpu_custom_call" | custom-call | tf_op jit(solution)/shard_map/pallas_call | solution.py:256
  28.1 0.6 %copy.10 = f32[2,1,1,2048]{3,2,1,0:T(1,128)} copy(f32[2,1,1,2048]{3,2,1,0:T(1,128)S(1)} %shard_map.73) | data formatting | bytes 32768
Async XLA Ops:
  0.7 1.2 %copy-start = (f32[1024,256]{1,0:T(8,128)S(1)}, f32[1024,256]{1,0:T(8,128)}, u32[]{:S(2)}) copy-start(f32[1024,256]{1,0:T(8,128)} %f_hbm.1) | copy-start | bytes 3145732
  1.9 1.1 %copy-start.1 = (bf16[768,512]{1,0:T(8,128)(2,1)S(1)}, bf16[768,512]{1,0:T(8,128)(2,1)}, u32[]{:S(2)}) copy-start(bf16[768,512]{1,0:T(8,128)(2,1)} %constant.8.clone.back_hbm) | copy-start | bytes 2359300
  3.0 0.9 %copy-start.2 = (f32[40,1024]{1,0:T(8,128)S(1)}, f32[40,1024]{1,0:T(8,128)}, u32[]{:S(2)}) copy-start(f32[40,1024]{1,0:T(8,128)} %constant.6.clone.tx_hbm) | copy-start | bytes 491524
  3.9 0.8 %copy-start.3 = (f32[56,256]{1,0:T(8,128)S(1)}, f32[56,256]{1,0:T(8,128)}, u32[]{:S(2)}) copy-start(f32[56,256]{1,0:T(8,128)} %constant.7.clone.ty_hbm) | copy-start | bytes 172036
  4.7 0.7 %copy-start.4 = (s32[2,1,1,2048]{3,2,1,0:T(1,128)S(1)}, s32[2,1,1,2048]{3,2,1,0:T(1,128)}, u32[]{:S(2)}) copy-start(s32[2,1,1,2048]{3,2,1,0:T(1,128)} %cells_hbm.1) | copy-start | bytes 49156
  5.5 0.7 %copy-start.5 = (f32[2,1,1,2048]{3,2,1,0:T(1,128)S(1)}, f32[2,1,1,2048]{3,2,1,0:T(1,128)}, u32[]{:S(2)}) copy-start(f32[2,1,1,2048]{3,2,1,0:T(1,128)} %fracs_hbm.1) | copy-start | bytes 49156

commit v2 on v1

v2 whole, which is shorter than its diff:
```python
import functools
import math

import jax
import jax.numpy as jnp
import numpy as np
from jax import lax
from jax.experimental import pallas as pl
from jax.experimental.pallas import tpu as pltpu
from jax.sharding import PartitionSpec as P

NIMG = 65536
FP = 4096
SUB = 256
SUPPORT = 8
VBLOCK = 128
MESH = pl.DeviceIdType.MESH
BF = jnp.bfloat16
F32 = jnp.float32


def separable(cells, pixels, rank):
    a = np.arange(cells) - (cells - 1) / 2
    b = np.arange(pixels) - (pixels - 1) / 2
    theta = 2 * np.pi * np.outer(a, b) / NIMG
    half = rank // 2
    uc, sc, vc = np.linalg.svd(np.cos(theta), full_matrices=False)
    us, ss, vs = np.linalg.svd(np.sin(theta), full_matrices=False)
    left = np.concatenate([uc[:, :half] * sc[:half], -1j * us[:, :half] * ss[:half]], axis=1)
    right = np.concatenate([vc[:half], vs[:half]], axis=0)
    norm = math.sqrt(pixels)
    return left / norm, right * norm


def axis_tables(parts, pixels, subs, rank):
    left, right = separable(SUB, pixels, rank)
    right = right * math.sqrt(2.0 / (parts * pixels))
    xx = np.arange(pixels)
    mid = SUB * np.arange(subs) + (SUB - 1) / 2
    phase = 2 * np.pi * ((mid[:, None] * xx[None, :]) / NIMG)
    turn = np.concatenate([np.cos(phase), -np.sin(phase)], axis=0)
    x = np.arange(parts * pixels)
    window = np.sin(np.pi * ((x % FP) + 0.5) / FP).reshape(parts, pixels)
    kk = np.arange(SUB)
    at = (kk[:, None] * np.arange(parts)[None, :] * pixels % NIMG) / NIMG
    at = at + ((kk - (SUB - 1) / 2) * ((pixels - 1) / 2) / NIMG)[:, None]
    back = np.exp(-2j * np.pi * at)[:, :, None] * left[:, None, :]
    return turn, right, window, back.reshape(SUB, parts * rank)


def split(x):
    high = x.astype(BF)
    return high, (x - high.astype(F32)).astype(BF)


def mm(a, b, dims):
    return lax.dot_general(a, b, (dims, ((), ())), preferred_element_type=F32)


def mm3(a, b, dims):
    (ah, al), (bh, bl) = a, b
    return mm(ah, bh, dims) + (mm(ah, bl, dims) + mm(al, bh, dims))


NN = ((1,), (0,))
NT = ((1,), (1,))
WIDE = 512
UNROLL = 4
FARX = (6, 5, 7, 2, 4, 1, 3)
FARY = (11, 10, 9, 8, 7, 6, 15, 14, 3, 2, 5, 4, 13, 12, 1)


def shift_x(at, d):
    return (at // 4 + d // 4) % 2 * 4 + (at + d) % 4


def shift_y(at, d):
    x = (at // 4 + d // 4) % 4
    near = (at // 2 + d // 2) % 2
    return x * 4 + near * 2 + (at + d) % 2


def weights(offset, frac, shape):
    cell = lax.broadcasted_iota(jnp.int32, shape, 0).astype(F32)
    shift = cell - (offset.astype(F32) + (SUPPORT // 2 - 1))
    inside = jnp.abs(shift - 0.5) < SUPPORT // 2
    shift = shift - frac
    value = 0.6 * jnp.exp(shift * shift * (-1.0 / 4.5))
    return jnp.where(inside, value, 0.0)


def kernel(
    nx, ny, rp, rq, tx_hbm, ty_hbm, back_hbm, f_hbm, counts_hbm, cells_hbm, fracs_hbm, out_ref,
    tx, ty, back, f, counts, cells, fracs, m2, z, r1, t, r2, wu, wv,
    fsem, lsem, s1, v1, s2, v2,
):
    me_x = lax.axis_index("fx")
    me_y = lax.axis_index("fy")
    rows = f.shape[0]
    cols = f.shape[1]
    step = rows // 4

    small = [
        pltpu.make_async_copy(src, dst, lsem.at[i])
        for i, (src, dst) in enumerate(
            [
                (tx_hbm, tx), (ty_hbm, ty), (cells_hbm, cells), (fracs_hbm, fracs),
                (counts_hbm, counts), (back_hbm, back),
            ]
        )
    ]
    big = [
        pltpu.make_async_copy(
            f_hbm.at[pl.ds(i * step, step)], f.at[pl.ds(i * step, step)], fsem.at[i]
        )
        for i in range(4)
    ]
    with jax.named_scope("a_start"):
        small[0].start()
        big[0].start()
        small[1].start()
        for copy in big[1:] + small[2:]:
            copy.start()

        barrier = pltpu.get_barrier_semaphore()
        for d in range(1, nx):
            pl.semaphore_signal(
                barrier, inc=1, device_id=(lax.rem(me_x + d, nx), me_y), device_id_type=MESH
            )
        for d in range(1, ny):
            pl.semaphore_signal(
                barrier, inc=1, device_id=(me_x, lax.rem(me_y + d, ny)), device_id_type=MESH
            )

    with jax.named_scope("b_c1"):
        small[0].wait()
        wx = tx[pl.ds(2 * nx + rp + me_x, 1), :]
        phi = tx[pl.ds(2 * nx, rp), :] * wx
        c1 = None
        for i in range(4):
            lanes = slice(i * step, (i + 1) * step)
            part = jnp.concatenate(
                [
                    jnp.broadcast_to(tx[pl.ds(r, 1), lanes], (rp, step)) * phi[:, lanes]
                    for r in range(2 * nx)
                ],
                axis=0,
            )
            big[i].wait()
            prod = mm3(split(part), split(f[pl.ds(i * step, step), :]), NN)
            c1 = prod if c1 is None else c1 + prod

    with jax.named_scope("c_d"):
        small[1].wait()
        wy = ty[pl.ds(2 * ny + rq + me_y, 1), :]
        phi = ty[pl.ds(2 * ny, rq), :] * wy
        for r in range(2 * ny):
            m2[pl.ds(r * rq, rq), :] = jnp.broadcast_to(ty[pl.ds(r, 1), :], (rq, cols)) * phi
        prod = mm3(split(c1), split(m2[...]), NT)
        hx = nx * rp
        hy = ny * rq
        z[0] = (prod[:hx, :hy] - prod[hx:, hy:]).reshape(nx, rp, hy)
        z[1] = (prod[:hx, hy:] + prod[hx:, :hy]).reshape(nx, rp, hy)

    with jax.named_scope("d_barrier"):
        pl.semaphore_wait(barrier, nx + ny - 2)
    first = []
    for d in FARX:
        peer = shift_x(me_x, d)
        copy = pltpu.make_async_remote_copy(
            src_ref=z.at[:, peer], dst_ref=r1.at[:, me_x], send_sem=s1.at[d], recv_sem=v1.at[d],
            device_id=(peer, me_y), device_id_type=MESH,
        )
        copy.start()
        first.append(copy)
    r1[:, pl.ds(me_x, 1)] = z[:, pl.ds(me_x, 1)]

    nvis = cells.shape[3]
    wide = WIDE
    kx = 2 * hx
    ky = 2 * hy

    def fill_u(j, carry):
        at = pl.ds(pl.multiple_of(j * wide, wide), wide)
        w = split(weights(cells[0, 0, :, at], fracs[0, 0, :, at], (SUB, wide)))
        high, low = split(mm3((back[:kx, :SUB], back[:kx, SUB:]), w, NN))
        wu[0, :, at] = high
        wu[1, :, at] = low
        return carry

    def fill_v(j, carry):
        at = pl.ds(pl.multiple_of(j * wide, wide), wide)
        w = split(weights(cells[1, 0, :, at], fracs[1, 0, :, at], (SUB, wide)))
        wv[:, at] = mm3((back[kx:, :SUB], back[kx:, SUB:]), w, NN)
        return carry

    with jax.named_scope("f_fillu"):
        for copy in small[2:]:
            copy.wait()
        lax.fori_loop(0, nvis // wide, fill_u, 0)

    with jax.named_scope("g_wait1"):
        for copy in first:
            copy.wait()
    with jax.named_scope("h_tr_send2"):
        for c in range(2):
            t[:, :, c * hx : (c + 1) * hx] = r1[c].reshape(hx, hy).T.reshape(ny, rq, hx)
    second = []
    for d in FARY:
        peer = shift_y(me_y, d)
        copy = pltpu.make_async_remote_copy(
            src_ref=t.at[peer], dst_ref=r2.at[me_y], send_sem=s2.at[d], recv_sem=v2.at[d],
            device_id=(me_x, peer), device_id_type=MESH,
        )
        copy.start()
        second.append(copy)
    r2[pl.ds(me_y, 1)] = t[pl.ds(me_y, 1)]

    with jax.named_scope("i_fillv"):
        lax.fori_loop(0, nvis // wide, fill_v, 0)
    with jax.named_scope("j_wait2"):
        for copy in second:
            copy.wait()

    with jax.named_scope("k_g"):
        got = r2[...].reshape(hy, kx)
        g_re = got[:, :hx]
        g_im = got[:, hx:]
        g = split(
            jnp.concatenate(
                [jnp.concatenate([g_re, -g_im], axis=1), jnp.concatenate([g_im, g_re], axis=1)],
                axis=0,
            )
        )
        live = counts[...]

    def degrid(j, carry):
        at = pl.ds(pl.multiple_of(j * wide, wide), wide)
        sums = mm3(g, (wu[0, :, at], wu[1, :, at]), NN)
        s_re, s_im = sums[:hy], sums[hy:]
        w_re, w_im = wv[:hy, at], wv[hy:, at]
        block = (lax.broadcasted_iota(jnp.int32, (1, wide), 1) + j * wide) // VBLOCK
        alive = block < live
        re = jnp.sum(s_re * w_re - s_im * w_im, axis=0, keepdims=True)
        im = jnp.sum(s_re * w_im + s_im * w_re, axis=0, keepdims=True)
        out_ref[0, 0, :, at] = jnp.where(alive, re, 0.0)
        out_ref[1, 0, :, at] = jnp.where(alive, im, 0.0)
        return carry

    with jax.named_scope("l_degrid"):
        lax.fori_loop(0, nvis // wide, degrid, 0, unroll=UNROLL)


def solution(mesh):
    nx = mesh.shape["fx"]
    ny = mesh.shape["fy"]
    rp, rq = 16, 8

    def per_device(facets, counts, cells, fracs):
        rows, cols = facets.shape
        nvis = cells.shape[3]
        turn_x, right_x, win_x, back_x = axis_tables(nx, rows, nx, rp)
        turn_y, right_y, win_y, back_y = axis_tables(ny, cols, ny, rq)
        tx = jnp.asarray(np.concatenate([turn_x, right_x, win_x]), F32)
        ty = jnp.asarray(np.concatenate([turn_y, right_y, win_y]), F32)
        back = np.concatenate([back_x.real, back_x.imag, back_y.real, back_y.imag], axis=1)
        back = np.ascontiguousarray(back.T).astype(np.float32)
        high = back.astype(BF)
        low = (back - high.astype(np.float32)).astype(BF)
        back = jnp.asarray(np.concatenate([high, low], axis=1))
        hx, hy = nx * rp, ny * rq
        any_spec = pl.BlockSpec(memory_space=pltpu.HBM)
        dma = pltpu.SemaphoreType.DMA
        return pl.pallas_call(
            functools.partial(kernel, nx, ny, rp, rq),
            out_shape=pltpu.VMEM((2, 1, 1, nvis), F32),
            in_specs=[any_spec] * 7,
            out_specs=pl.BlockSpec(memory_space=pltpu.VMEM),
            scratch_shapes=[
                pltpu.VMEM(tx.shape, F32),
                pltpu.VMEM(ty.shape, F32),
                pltpu.VMEM(back.shape, BF),
                pltpu.VMEM((rows, cols), F32),
                pltpu.VMEM((1, 1), jnp.int32),
                pltpu.VMEM(cells.shape, jnp.int32),
                pltpu.VMEM(fracs.shape, F32),
                pltpu.VMEM((2 * hy, cols), F32),
                pltpu.VMEM((2, nx, rp, hy), F32),
                pltpu.VMEM((2, nx, rp, hy), F32),
                pltpu.VMEM((ny, rq, 2 * hx), F32),
                pltpu.VMEM((ny, rq, 2 * hx), F32),
                pltpu.VMEM((2, 2 * hx, nvis), BF),
                pltpu.VMEM((2 * hy, nvis), F32),
                dma((4,)),
                dma((6,)),
                dma((nx,)),
                dma((nx,)),
                dma((ny,)),
                dma((ny,)),
            ],
            compiler_params=pltpu.CompilerParams(
                collective_id=0, has_side_effects=True
            ),
        )(tx, ty, back, facets, counts, cells, fracs)

    spec = P(None, "fx", "fy", None)
    return jax.shard_map(
        per_device,
        mesh=mesh,
        in_specs=(P("fx", "fy"), P("fx", "fy"), spec, spec),
        out_specs=spec,
        check_vma=False,
    )
```

time: 29 us -> 20.3 us (0.70)
  local copies, waits for them, and re-layouts: 6.13 us -> 0.61 us
  Pallas kernels: 21.9 us -> 18.9 us
    unnamed x13 -> x1, local copies, waits for them, and re-layouts: 6.13 us -> 0.61 us
    pallas_call x1, Pallas kernels: 21.9 us -> 18.9 us  [per_device(): pl.pallas_call(functools.partial(kernel, nx, ny, rp, rq), out_shape=pltpu...]
where the time goes in v2:
time: 20.3 us; the launch traced here: 20.1 us
  Pallas kernels  18.9 us (93%)
  between operations  0.66 us (3%)
  local copies, waits for them, and re-layouts  0.61 us (3%)
    pallas_call x1, Pallas kernels, per_device(): pl.pallas_call(functools.partial(kernel, nx, ny, rp, rq), out_shape=pltpu...  18.9 us
    unnamed x1, local copies, waits for them, and re-layouts  0.61 us

profile of v2, /device:TPU:1, one launch (start us, length us, event | category | flops | bytes accessed | tf_op | source)
XLA Modules:
  0.0 20.1 jit_solution(8830041170523441817)
XLA Ops:
  0.7 18.9 %shard_map.73 = f32[2,1,1,2048]{3,2,1,0:T(1,128)S(1)} custom-call(f32[40,1024]{1,0:T(8,128)} %constant.6.clone.tx_hbm, f32[56,256]{1,0:T(8,128)} %constant.7.clone.ty_hbm, bf16[512,512]{1,0:T(8,128)(2,1)} %constant.8.clone.back_hbm, f32[1024,256]{1,0:T(8,128)} %f_hbm.1, s32[1,1]{1,0:T(1,128)S(6)} %copy.10.counts_hbm, s32[2,1,1,2048]{3,2,1,0:T(1,128)} %cells_hbm.1, ...), custom_call_target="tpu_custom_call" | custom-call | tf_op jit(solution)/shard_map/pallas_call | solution.py:274
  19.5 0.6 %copy.9 = f32[2,1,1,2048]{3,2,1,0:T(1,128)} copy(f32[2,1,1,2048]{3,2,1,0:T(1,128)S(1)} %shard_map.73) | data formatting | bytes 32768

commit v3 on v2

--- a/solution.py
+++ b/solution.py
@@ -14,7 +14,7 @@
 SUB = 256
 SUPPORT = 8
 VBLOCK = 128
-MESH = pl.DeviceIdType.MESH
+LOGICAL = pl.DeviceIdType.LOGICAL
 BF = jnp.bfloat16
 F32 = jnp.float32
 
@@ -64,20 +64,36 @@
 
 NN = ((1,), (0,))
 NT = ((1,), (1,))
+
 WIDE = 512
-UNROLL = 4
-FARX = (6, 5, 7, 2, 4, 1, 3)
-FARY = (11, 10, 9, 8, 7, 6, 15, 14, 3, 2, 5, 4, 13, 12, 1)
-
-
-def shift_x(at, d):
-    return (at // 4 + d // 4) % 2 * 4 + (at + d) % 4
-
-
-def shift_y(at, d):
-    x = (at // 4 + d // 4) % 4
-    near = (at // 2 + d // 2) % 2
-    return x * 4 + near * 2 + (at + d) % 2
+PEERS = sorted(
+    ((a, b) for a in range(8) for b in range(16) if a or b),
+    key=lambda o: -(
+        2 * (o[0] // 4) + (0, 1, 2, 1)[o[0] % 4] + (0, 1, 2, 1)[o[1] // 4] + (o[1] // 2) % 2
+    ),
+)
+
+
+def swap_blocks(x, size):
+    shape = (x.shape[0], 8, x.shape[2])
+    lane = lax.broadcasted_iota(jnp.int32, shape, 2) // size
+    row = lax.broadcasted_iota(jnp.int32, shape, 1)
+    width = x.shape[2]
+    top, low = x[:, :8], x[:, 8:]
+    left = lane < 8
+    halves = [
+        jnp.where(left, top, pltpu.roll(low, width // 2, 2)),
+        jnp.where(left, pltpu.roll(top, width // 2, 2), low),
+    ]
+    for d in (4, 2, 1):
+        up = (row // d) % 2
+        same = up == (lane // d) % 2
+        for h in range(2):
+            v = halves[h]
+            right = pltpu.roll(pltpu.roll(v, 8 - d, 1), size * d, 2)
+            back = pltpu.roll(pltpu.roll(v, d, 1), width - size * d, 2)
+            halves[h] = jnp.where(same, v, jnp.where(up == 0, right, back))
+    return jnp.concatenate(halves, axis=1)
 
 
 def weights(offset, frac, shape):
@@ -91,8 +107,8 @@
 
 def kernel(
     nx, ny, rp, rq, tx_hbm, ty_hbm, back_hbm, f_hbm, counts_hbm, cells_hbm, fracs_hbm, out_ref,
-    tx, ty, back, f, counts, cells, fracs, m2, z, r1, t, r2, wu, wv,
-    fsem, lsem, s1, v1, s2, v2,
+    tx, ty, back, f, counts, cells, fracs, m2, z, got, wv, wu,
+    fsem, lsem, sent, came,
 ):
     me_x = lax.axis_index("fx")
     me_y = lax.axis_index("fy")
@@ -122,14 +138,15 @@
         for copy in big[1:] + small[2:]:
             copy.start()
 
+        at_x = [((me_x // 4 + a // 4) % 2 * 4 + (me_x + a) % 4) * ny for a in range(nx)]
+        at_y = [
+            (me_y // 4 + b // 4) % 4 * 4 + (me_y // 2 + b // 2) % 2 * 2 + (me_y + b) % 2
+            for b in range(ny)
+        ]
         barrier = pltpu.get_barrier_semaphore()
-        for d in range(1, nx):
+        for a, b in PEERS:
             pl.semaphore_signal(
-                barrier, inc=1, device_id=(lax.rem(me_x + d, nx), me_y), device_id_type=MESH
-            )
-        for d in range(1, ny):
-            pl.semaphore_signal(
-                barrier, inc=1, device_id=(me_x, lax.rem(me_y + d, ny)), device_id_type=MESH
+                barrier, inc=1, device_id=at_x[a] + at_y[b], device_id_type=LOGICAL
             )
 
     with jax.named_scope("b_c1"):
@@ -159,73 +176,60 @@
         prod = mm3(split(c1), split(m2[...]), NT)
         hx = nx * rp
         hy = ny * rq
-        z[0] = (prod[:hx, :hy] - prod[hx:, hy:]).reshape(nx, rp, hy)
-        z[1] = (prod[:hx, hy:] + prod[hx:, :hy]).reshape(nx, rp, hy)
+        re = prod[:hx, :hy] - prod[hx:, hy:]
+        im = prod[:hx, hy:] + prod[hx:, :hy]
+        both = swap_blocks(jnp.concatenate([re, im]).reshape(2 * nx, rp, hy), rq)
+        z[:, 0, :] = both[:nx].reshape(nx * ny, hy)
+        z[:, 1, :] = both[nx:].reshape(nx * ny, hy)
 
     with jax.named_scope("d_barrier"):
-        pl.semaphore_wait(barrier, nx + ny - 2)
-    first = []
-    for d in FARX:
-        peer = shift_x(me_x, d)
-        copy = pltpu.make_async_remote_copy(
-            src_ref=z.at[:, peer], dst_ref=r1.at[:, me_x], send_sem=s1.at[d], recv_sem=v1.at[d],
-            device_id=(peer, me_y), device_id_type=MESH,
-        )
-        copy.start()
-        first.append(copy)
-    r1[:, pl.ds(me_x, 1)] = z[:, pl.ds(me_x, 1)]
+        pl.semaphore_wait(barrier, nx * ny - 1)
+    with jax.named_scope("e_send"):
+        me = me_x * ny + me_y
+        for a, b in PEERS:
+            peer = at_x[a] + at_y[b]
+            pltpu.make_async_remote_copy(
+                src_ref=z.at[peer], dst_ref=got.at[me], send_sem=sent, recv_sem=came,
+                device_id=peer, device_id_type=LOGICAL,
+            ).start()
+        got[pl.ds(me, 1)] = z[pl.ds(me, 1)]
 
     nvis = cells.shape[3]
     wide = WIDE
     kx = 2 * hx
     ky = 2 * hy
 
+    def fill_v(j, carry):
+        at = pl.ds(pl.multiple_of(j * wide, wide), wide)
+        w = split(weights(cells[1, 0, :, at], fracs[1, 0, :, at], (SUB, wide)))
+        high, low = split(mm3((back[kx:, :SUB], back[kx:, SUB:]), w, NN))
+        wv[0, :, at] = high
+        wv[1, :, at] = low
+        return carry
+
     def fill_u(j, carry):
         at = pl.ds(pl.multiple_of(j * wide, wide), wide)
         w = split(weights(cells[0, 0, :, at], fracs[0, 0, :, at], (SUB, wide)))
-        high, low = split(mm3((back[:kx, :SUB], back[:kx, SUB:]), w, NN))
-        wu[0, :, at] = high
-        wu[1, :, at] = low
+        wu[:, at] = mm3((back[:kx, :SUB], back[:kx, SUB:]), w, NN)
         return carry
 
-    def fill_v(j, carry):
-        at = pl.ds(pl.multiple_of(j * wide, wide), wide)
-        w = split(weights(cells[1, 0, :, at], fracs[1, 0, :, at], (SUB, wide)))
-        wv[:, at] = mm3((back[kx:, :SUB], back[kx:, SUB:]), w, NN)
-        return carry
-
-    with jax.named_scope("f_fillu"):
+    with jax.named_scope("f_fill"):
         for copy in small[2:]:
             copy.wait()
+        lax.fori_loop(0, nvis // wide, fill_v, 0)
         lax.fori_loop(0, nvis // wide, fill_u, 0)
 
-    with jax.named_scope("g_wait1"):
-        for copy in first:
-            copy.wait()
-    with jax.named_scope("h_tr_send2"):
-        for c in range(2):
-            t[:, :, c * hx : (c + 1) * hx] = r1[c].reshape(hx, hy).T.reshape(ny, rq, hx)
-    second = []
-    for d in FARY:
-        peer = shift_y(me_y, d)
-        copy = pltpu.make_async_remote_copy(
-            src_ref=t.at[peer], dst_ref=r2.at[me_y], send_sem=s2.at[d], recv_sem=v2.at[d],
-            device_id=(me_x, peer), device_id_type=MESH,
+    with jax.named_scope("g_wait"):
+        others = pl.ds(0, nx * ny - 1)
+        every = pltpu.make_async_remote_copy(
+            src_ref=z.at[others], dst_ref=got.at[others], send_sem=sent, recv_sem=came,
+            device_id=me, device_id_type=LOGICAL,
         )
-        copy.start()
-        second.append(copy)
-    r2[pl.ds(me_y, 1)] = t[pl.ds(me_y, 1)]
-
-    with jax.named_scope("i_fillv"):
-        lax.fori_loop(0, nvis // wide, fill_v, 0)
-    with jax.named_scope("j_wait2"):
-        for copy in second:
-            copy.wait()
+        every.wait()
 
     with jax.named_scope("k_g"):
-        got = r2[...].reshape(hy, kx)
-        g_re = got[:, :hx]
-        g_im = got[:, hx:]
+        g_re = swap_blocks(got[:, 0, :].reshape(nx, ny, hy), rq).reshape(hx, hy)
+        g_im = swap_blocks(got[:, 1, :].reshape(nx, ny, hy), rq).reshape(hx, hy)
         g = split(
             jnp.concatenate(
                 [jnp.concatenate([g_re, -g_im], axis=1), jnp.concatenate([g_im, g_re], axis=1)],
@@ -236,9 +240,9 @@
 
     def degrid(j, carry):
         at = pl.ds(pl.multiple_of(j * wide, wide), wide)
-        sums = mm3(g, (wu[0, :, at], wu[1, :, at]), NN)
-        s_re, s_im = sums[:hy], sums[hy:]
-        w_re, w_im = wv[:hy, at], wv[hy:, at]
+        sums = mm3(g, (wv[0, :, at], wv[1, :, at]), NN)
+        s_re, s_im = sums[:hx], sums[hx:]
+        w_re, w_im = wu[:hx, at], wu[hx:, at]
         block = (lax.broadcasted_iota(jnp.int32, (1, wide), 1) + j * wide) // VBLOCK
         alive = block < live
         re = jnp.sum(s_re * w_re - s_im * w_im, axis=0, keepdims=True)
@@ -248,7 +252,7 @@
         return carry
 
     with jax.named_scope("l_degrid"):
-        lax.fori_loop(0, nvis // wide, degrid, 0, unroll=UNROLL)
+        lax.fori_loop(0, nvis // wide, degrid, 0, unroll=4)
 
 
 def solution(mesh):
@@ -285,18 +289,14 @@
                 pltpu.VMEM(cells.shape, jnp.int32),
                 pltpu.VMEM(fracs.shape, F32),
                 pltpu.VMEM((2 * hy, cols), F32),
-                pltpu.VMEM((2, nx, rp, hy), F32),
-                pltpu.VMEM((2, nx, rp, hy), F32),
-                pltpu.VMEM((ny, rq, 2 * hx), F32),
-                pltpu.VMEM((ny, rq, 2 * hx), F32),
-                pltpu.VMEM((2, 2 * hx, nvis), BF),
-                pltpu.VMEM((2 * hy, nvis), F32),
+                pltpu.VMEM((nx * ny, 2, hy), F32),
+                pltpu.VMEM((nx * ny, 2, hy), F32),
+                pltpu.VMEM((2, 2 * hy, nvis), BF),
+                pltpu.VMEM((2 * hx, nvis), F32),
                 dma((4,)),
                 dma((6,)),
-                dma((nx,)),
-                dma((nx,)),
-                dma((ny,)),
-                dma((ny,)),
+                dma,
+                dma,
             ],
             compiler_params=pltpu.CompilerParams(
                 collective_id=0, has_side_effects=True

time: 20.3 us -> 19 us (0.936)
  Pallas kernels: 18.9 us -> 17.6 us
    pallas_call x1, Pallas kernels: 18.9 us -> 17.6 us  [per_device(): pl.pallas_call(functools.partial(kernel, nx, ny, rp, rq), out_shape=pltpu...]
where the time goes in v3:
time: 19 us; the launch traced here: 18.9 us
  Pallas kernels  17.6 us (93%)
  between operations  0.66 us (3%)
  local copies, waits for them, and re-layouts  0.61 us (3%)
    pallas_call x1, Pallas kernels, per_device(): pl.pallas_call(functools.partial(kernel, nx, ny, rp, rq), out_shape=pltpu...  17.6 us
    unnamed x1, local copies, waits for them, and re-layouts  0.61 us

profile of v3, /device:TPU:1, one launch (start us, length us, event | category | flops | bytes accessed | tf_op | source)
XLA Modules:
  0.0 18.9 jit_solution(7324411767669715103)
XLA Ops:
  0.7 17.6 %shard_map.73 = f32[2,1,1,2048]{3,2,1,0:T(1,128)S(1)} custom-call(f32[40,1024]{1,0:T(8,128)} %constant.6.clone.tx_hbm, f32[56,256]{1,0:T(8,128)} %constant.7.clone.ty_hbm, bf16[512,512]{1,0:T(8,128)(2,1)} %constant.8.clone.back_hbm, f32[1024,256]{1,0:T(8,128)} %f_hbm.1, s32[1,1]{1,0:T(1,128)S(6)} %copy.10.counts_hbm, s32[2,1,1,2048]{3,2,1,0:T(1,128)} %cells_hbm.1, ...), custom_call_target="tpu_custom_call" | custom-call | tf_op jit(solution)/shard_map/pallas_call | solution.py:278
  18.3 0.6 %copy.9 = f32[2,1,1,2048]{3,2,1,0:T(1,128)} copy(f32[2,1,1,2048]{3,2,1,0:T(1,128)S(1)} %shard_map.73) | data formatting | bytes 32768

commit v4 on v3

v4 whole, which is shorter than its diff:
```python
import functools
import math

import jax
import jax.numpy as jnp
import numpy as np
from jax import lax
from jax.experimental import pallas as pl
from jax.experimental.pallas import tpu as pltpu
from jax.sharding import PartitionSpec as P

NIMG = 65536
FP = 4096
SUB = 256
SUPPORT = 8
VBLOCK = 128
LOGICAL = pl.DeviceIdType.LOGICAL
BF = jnp.bfloat16
F32 = jnp.float32


def separable(cells, pixels, rank):
    a = np.arange(cells) - (cells - 1) / 2
    b = np.arange(pixels) - (pixels - 1) / 2
    theta = 2 * np.pi * np.outer(a, b) / NIMG
    half = rank // 2
    uc, sc, vc = np.linalg.svd(np.cos(theta), full_matrices=False)
    us, ss, vs = np.linalg.svd(np.sin(theta), full_matrices=False)
    left = np.concatenate([uc[:, :half] * sc[:half], -1j * us[:, :half] * ss[:half]], axis=1)
    right = np.concatenate([vc[:half], vs[:half]], axis=0)
    norm = math.sqrt(pixels)
    return left / norm, right * norm


def axis_tables(parts, pixels, subs, rank):
    left, right = separable(SUB, pixels, rank)
    right = right * math.sqrt(2.0 / (parts * pixels))
    xx = np.arange(pixels)
    mid = SUB * np.arange(subs) + (SUB - 1) / 2
    phase = 2 * np.pi * ((mid[:, None] * xx[None, :]) / NIMG)
    turn = np.concatenate([np.cos(phase), -np.sin(phase)], axis=0)
    x = np.arange(parts * pixels)
    window = np.sin(np.pi * ((x % FP) + 0.5) / FP).reshape(parts, pixels)
    kk = np.arange(SUB)
    at = (kk[:, None] * np.arange(parts)[None, :] * pixels % NIMG) / NIMG
    at = at + ((kk - (SUB - 1) / 2) * ((pixels - 1) / 2) / NIMG)[:, None]
    back = np.exp(-2j * np.pi * at)[:, :, None] * left[:, None, :]
    return turn, right, window, back.reshape(SUB, parts * rank)


def split(x):
    high = x.astype(BF)
    return high, (x - high.astype(F32)).astype(BF)


def halves(table, axis):
    table = table.astype(np.float32)
    high = table.astype(BF)
    low = (table - high.astype(np.float32)).astype(BF)
    return jnp.asarray(np.concatenate([high, low], axis=axis))


def mm(a, b, dims):
    return lax.dot_general(a, b, (dims, ((), ())), preferred_element_type=F32)


def mm3(a, b, dims):
    (ah, al), (bh, bl) = a, b
    return mm(ah, bh, dims) + (mm(ah, bl, dims) + mm(al, bh, dims))


NN = ((1,), (0,))
NT = ((1,), (1,))

WIDE = 512
RANK_X = 88
RANK_Y = 48


def place(k):
    return (k // 4 % 4, k // 64 * 2 + k // 2 % 2, k // 16 % 4, k % 2)


def hops(k):
    x, y, z, _ = place(k)
    return sum(min(c, 4 - c) for c in (x, y, z))


def launch_order(k):
    x, y, z, core = place(k)
    return ((z * 4 + y) * 4 + x, 1 - core)


SENDS = sorted(range(128), key=launch_order)
SIGNALS = sorted(range(128), key=lambda k: (-hops(k), launch_order(k)))


def compress(back, rank):
    terms = back.shape[1]
    u, s, v = np.linalg.svd(np.concatenate([back.real, back.imag], axis=1), full_matrices=False)
    rest = s[:rank, None] * v[:rank]
    return u[:, :rank], rest[:, :terms], rest[:, terms:]


def swap_blocks(parts, size):
    parts = list(parts)
    width = parts[0].shape[1]
    lane = lax.broadcasted_iota(jnp.int32, parts[0].shape, 1) // size
    d = len(parts) // 2
    while d:
        low = (lane // d) % 2 == 0
        for p in range(len(parts)):
            if p // d % 2 == 0:
                a, b = parts[p], parts[p + d]
                parts[p] = jnp.where(low, a, pltpu.roll(b, size * d, 1))
                parts[p + d] = jnp.where(low, pltpu.roll(a, width - size * d, 1), b)
        d //= 2
    return parts


def weights(offset, frac, shape):
    cell = lax.broadcasted_iota(jnp.int32, shape, 0).astype(F32)
    shift = cell - (offset.astype(F32) + (SUPPORT // 2 - 1))
    inside = jnp.abs(shift - 0.5) < SUPPORT // 2
    shift = shift - frac
    value = 0.6 * jnp.exp(shift * shift * (-1.0 / 4.5))
    return jnp.where(inside, value, 0.0)


def kernel(
    nx, ny, rp, rq, tx_hbm, ty_hbm, cell_hbm, rx_hbm, ry_hbm, f_hbm, counts_hbm, cells_hbm, fracs_hbm, out_ref,
    tx, ty, cell, rx, ry, f, counts, cells, fracs, m2, z, got, wv, wu,
    fsem, lsem, sent, came,
):
    me_x = lax.axis_index("fx")
    me_y = lax.axis_index("fy")
    rows = f.shape[0]
    cols = f.shape[1]
    step = rows // 4

    small = [
        pltpu.make_async_copy(src, dst, lsem.at[i])
        for i, (src, dst) in enumerate(
            [
                (tx_hbm, tx), (ty_hbm, ty), (cells_hbm, cells), (fracs_hbm, fracs),
                (counts_hbm, counts), (cell_hbm, cell), (rx_hbm, rx), (ry_hbm, ry),
            ]
        )
    ]
    big = [
        pltpu.make_async_copy(
            f_hbm.at[pl.ds(i * step, step)], f.at[pl.ds(i * step, step)], fsem.at[i]
        )
        for i in range(4)
    ]
    with jax.named_scope("a_start"):
        small[0].start()
        big[0].start()
        small[1].start()
        for copy in big[1:] + small[2:]:
            copy.start()

        barrier = pltpu.get_barrier_semaphore()
        me = me_x * ny + me_y
        for k in SIGNALS:

            @pl.when(me != k)
            def _():
                pl.semaphore_signal(barrier, inc=1, device_id=k, device_id_type=LOGICAL)

    with jax.named_scope("b_c1"):
        small[0].wait()
        wx = tx[pl.ds(2 * nx + rp + me_x, 1), :]
        phi = tx[pl.ds(2 * nx, rp), :] * wx
        c1 = None
        for i in range(4):
            lanes = slice(i * step, (i + 1) * step)
            part = jnp.concatenate(
                [
                    tx[c * nx : (c + 1) * nx, lanes] * phi[p : p + 1, lanes]
                    for c in range(2)
                    for p in range(rp)
                ],
                axis=0,
            )
            big[i].wait()
            prod = mm3(split(part), split(f[pl.ds(i * step, step), :]), NN)
            c1 = prod if c1 is None else c1 + prod

    with jax.named_scope("c_d"):
        small[1].wait()
        wy = ty[pl.ds(2 * ny + rq + me_y, 1), :]
        phi = ty[pl.ds(2 * ny, rq), :] * wy
        for r in range(2 * ny):
            m2[pl.ds(r * rq, rq), :] = jnp.broadcast_to(ty[pl.ds(r, 1), :], (rq, cols)) * phi
        prod = mm3(split(c1), split(m2[...]), NT)
        hx = nx * rp
        hy = ny * rq
        re = prod[:hx, :hy] - prod[hx:, hy:]
        im = prod[:hx, hy:] + prod[hx:, :hy]
        for c, part in enumerate((re, im)):
            swapped = swap_blocks([part[p * nx : (p + 1) * nx] for p in range(rp)], rq)
            for v in range(ny):
                z[v * nx : (v + 1) * nx, c, :] = swapped[v]

    nvis = cells.shape[3]
    wide = WIDE
    kx = rx.shape[0] // 2
    ky = cell.shape[0] - kx

    def fill_v(j, carry):
        at = pl.ds(pl.multiple_of(j * wide, wide), wide)
        w = split(weights(cells[1, 0, :, at], fracs[1, 0, :, at], (SUB, wide)))
        high, low = split(mm3((cell[kx:, :SUB], cell[kx:, SUB:]), w, NN))
        wv[:ky, at] = high
        wv[ky : 2 * ky, at] = high
        wv[2 * ky :, at] = low
        return carry

    def fill_u(j, carry):
        at = pl.ds(pl.multiple_of(j * wide, wide), wide)
        w = split(weights(cells[0, 0, :, at], fracs[0, 0, :, at], (SUB, wide)))
        wu[:, at] = mm3((cell[:kx, :SUB], cell[:kx, SUB:]), w, NN)
        return carry

    chunks = nvis // wide
    early = lax.div(3 - lax.rem(me_x, 4), 3) * chunks
    with jax.named_scope("c_fill"):
        for copy in small[2:]:
            copy.wait()
        lax.fori_loop(0, early, fill_v, 0)

    with jax.named_scope("d_barrier"):
        pl.semaphore_wait(barrier, nx * ny - 1)
    with jax.named_scope("e_send"):
        slot = me_y * nx + me_x
        for k in SENDS:

            @pl.when(me != k)
            def _():
                pltpu.make_async_remote_copy(
                    src_ref=z.at[k % ny * nx + k // ny], dst_ref=got.at[slot],
                    send_sem=sent, recv_sem=came, device_id=k, device_id_type=LOGICAL,
                ).start()

        got[pl.ds(slot, 1)] = z[pl.ds(slot, 1)]

    with jax.named_scope("f_fill"):
        lax.fori_loop(early, chunks, fill_v, 0)
        lax.fori_loop(0, chunks, fill_u, 0)

    with jax.named_scope("g_wait"):
        others = pl.ds(0, nx * ny - 1)
        every = pltpu.make_async_remote_copy(
            src_ref=z.at[others], dst_ref=got.at[others], send_sem=sent, recv_sem=came,
            device_id=me, device_id_type=LOGICAL,
        )
        every.wait()

    with jax.named_scope("k_g"):
        g_re, g_im = (
            jnp.concatenate(
                swap_blocks([got[v * nx : (v + 1) * nx, c, :] for v in range(ny)], rq)
            )
            for c in range(2)
        )
        g = split(
            jnp.concatenate(
                [jnp.concatenate([g_re, -g_im], axis=1), jnp.concatenate([g_im, g_re], axis=1)],
                axis=0,
            )
        )
        g = split(mm3(g, (ry[0], ry[1]), NN))
        g = mm3((rx[:, : 2 * hx], rx[:, 2 * hx :]), g, NN)
        high, low = split(g)
        copy_of = lax.broadcasted_iota(jnp.int32, g.shape, 1) // ky
        g = jnp.where(copy_of == 1, low.astype(F32), high.astype(F32)).astype(BF)
        live = counts[...]

    def degrid(j, carry):
        at = pl.ds(pl.multiple_of(j * wide, wide), wide)
        sums = mm(g, wv[:, at], NN)
        w = wu[:, at]
        block = (lax.broadcasted_iota(jnp.int32, (1, wide), 1) + j * wide) // VBLOCK
        alive = block < live
        re = jnp.sum(sums[:kx] * w, axis=0, keepdims=True)
        im = jnp.sum(sums[kx:] * w, axis=0, keepdims=True)
        out_ref[0, 0, :, at] = jnp.where(alive, re, 0.0)
        out_ref[1, 0, :, at] = jnp.where(alive, im, 0.0)
        return carry

    with jax.named_scope("l_degrid"):
        lax.fori_loop(0, nvis // wide, degrid, 0, unroll=4)


def solution(mesh):
    nx = mesh.shape["fx"]
    ny = mesh.shape["fy"]
    rp, rq = 16, 8

    def per_device(facets, counts, cells, fracs):
        rows, cols = facets.shape
        nvis = cells.shape[3]
        turn_x, right_x, win_x, back_x = axis_tables(nx, rows, nx, rp)
        turn_y, right_y, win_y, back_y = axis_tables(ny, cols, ny, rq)
        tx = jnp.asarray(np.concatenate([turn_x, right_x, win_x]), F32)
        ty = jnp.asarray(np.concatenate([turn_y, right_y, win_y]), F32)
        back_x = back_x.reshape(SUB, nx, rp).swapaxes(1, 2).reshape(SUB, nx * rp)
        base_x, re_x, im_x = compress(back_x, RANK_X)
        base_y, re_y, im_y = compress(back_y, RANK_Y)
        cell = halves(np.concatenate([base_x.T, base_y.T]), 1)
        rx = halves(
            np.concatenate(
                [np.concatenate([re_x, -im_x], axis=1), np.concatenate([im_x, re_x], axis=1)]
            ),
            1,
        )
        ry = np.concatenate([re_y, im_y], axis=1).T
        ry = halves(np.concatenate([ry, ry, ry], axis=1)[None], 0)
        hx, hy = nx * rp, ny * rq
        any_spec = pl.BlockSpec(memory_space=pltpu.HBM)
        dma = pltpu.SemaphoreType.DMA
        return pl.pallas_call(
            functools.partial(kernel, nx, ny, rp, rq),
            out_shape=pltpu.VMEM((2, 1, 1, nvis), F32),
            in_specs=[any_spec] * 9,
            out_specs=pl.BlockSpec(memory_space=pltpu.VMEM),
            scratch_shapes=[
                pltpu.VMEM(tx.shape, F32),
                pltpu.VMEM(ty.shape, F32),
                pltpu.VMEM(cell.shape, BF),
                pltpu.VMEM(rx.shape, BF),
                pltpu.VMEM(ry.shape, BF),
                pltpu.VMEM((rows, cols), F32),
                pltpu.VMEM((1, 1), jnp.int32),
                pltpu.VMEM(cells.shape, jnp.int32),
                pltpu.VMEM(fracs.shape, F32),
                pltpu.VMEM((2 * hy, cols), F32),
                pltpu.VMEM((nx * ny, 2, hy), F32),
                pltpu.VMEM((nx * ny, 2, hy), F32),
                pltpu.VMEM((3 * RANK_Y, nvis), BF),
                pltpu.VMEM((RANK_X, nvis), F32),
                dma((4,)),
                dma((8,)),
                dma,
                dma,
            ],
            compiler_params=pltpu.CompilerParams(
                collective_id=0, has_side_effects=True
            ),
        )(tx, ty, cell, rx, ry, facets, counts, cells, fracs)

    spec = P(None, "fx", "fy", None)
    return jax.shard_map(
        per_device,
        mesh=mesh,
        in_specs=(P("fx", "fy"), P("fx", "fy"), spec, spec),
        out_specs=spec,
        check_vma=False,
    )
```

time: 19 us -> 17.4 us (0.916)
  Pallas kernels: 17.6 us -> 16 us
    pallas_call x1, Pallas kernels: 17.6 us -> 16 us  [per_device(): pl.pallas_call(functools.partial(kernel, nx, ny, rp, rq), out_shape=pltpu...]
where the time goes in v4:
time: 17.4 us; the launch traced here: 17.3 us
  Pallas kernels  16 us (92%)
  between operations  0.66 us (4%)
  local copies, waits for them, and re-layouts  0.61 us (4%)
    pallas_call x1, Pallas kernels, per_device(): pl.pallas_call(functools.partial(kernel, nx, ny, rp, rq), out_shape=pltpu...  16 us
    unnamed x1, local copies, waits for them, and re-layouts  0.61 us

profile of v4, /device:TPU:1, one launch (start us, length us, event | category | flops | bytes accessed | tf_op | source)
XLA Modules:
  0.0 17.3 jit_solution(5582053309833442597)
XLA Ops:
  0.7 16.0 %shard_map.91 = f32[2,1,1,2048]{3,2,1,0:T(1,128)S(1)} custom-call(f32[40,1024]{1,0:T(8,128)} %constant.10.clone.tx_hbm, f32[56,256]{1,0:T(8,128)} %constant.11.clone.ty_hbm, bf16[136,512]{1,0:T(8,128)(2,1)} %constant.12.clone.cell_hbm, bf16[176,512]{1,0:T(8,128)(2,1)} %constant.13.clone.rx_hbm, bf16[2,256,144]{2,1,0:T(8,128)(2,1)} %constant.14.clone.ry_hbm, ...), custom_call_target="tpu_custom_call" | custom-call | tf_op jit(solution)/shard_map/pallas_call | solution.py:323
  16.7 0.6 %copy.11 = f32[2,1,1,2048]{3,2,1,0:T(1,128)} copy(f32[2,1,1,2048]{3,2,1,0:T(1,128)S(1)} %shard_map.91) | data formatting | bytes 32768

commit v5 on v4

--- a/solution.py
+++ b/solution.py
@@ -73,7 +73,7 @@
 NT = ((1,), (1,))
 
 WIDE = 512
-RANK_X = 88
+RANK_X = 80
 RANK_Y = 48
 
 
@@ -129,7 +129,7 @@
 
 def kernel(
     nx, ny, rp, rq, tx_hbm, ty_hbm, cell_hbm, rx_hbm, ry_hbm, f_hbm, counts_hbm, cells_hbm, fracs_hbm, out_ref,
-    tx, ty, cell, rx, ry, f, counts, cells, fracs, m2, z, got, wv, wu,
+    tx, ty, cell, rx, ry, f, counts, cells, fracs, m2, z, got, wu, wv,
     fsem, lsem, sent, came,
 ):
     me_x = lax.axis_index("fx")
@@ -205,22 +205,22 @@
 
     nvis = cells.shape[3]
     wide = WIDE
-    kx = rx.shape[0] // 2
-    ky = cell.shape[0] - kx
+    kx = RANK_X
+    ky = RANK_Y
+
+    def fill_u(j, carry):
+        at = pl.ds(pl.multiple_of(j * wide, wide), wide)
+        w = split(weights(cells[0, 0, :, at], fracs[0, 0, :, at], (SUB, wide)))
+        high, low = split(mm3((cell[:kx, :SUB], cell[:kx, SUB:]), w, NN))
+        wu[:kx, at] = high
+        wu[kx : 2 * kx, at] = high
+        wu[2 * kx :, at] = low
+        return carry
 
     def fill_v(j, carry):
         at = pl.ds(pl.multiple_of(j * wide, wide), wide)
         w = split(weights(cells[1, 0, :, at], fracs[1, 0, :, at], (SUB, wide)))
-        high, low = split(mm3((cell[kx:, :SUB], cell[kx:, SUB:]), w, NN))
-        wv[:ky, at] = high
-        wv[ky : 2 * ky, at] = high
-        wv[2 * ky :, at] = low
-        return carry
-
-    def fill_u(j, carry):
-        at = pl.ds(pl.multiple_of(j * wide, wide), wide)
-        w = split(weights(cells[0, 0, :, at], fracs[0, 0, :, at], (SUB, wide)))
-        wu[:, at] = mm3((cell[:kx, :SUB], cell[:kx, SUB:]), w, NN)
+        wv[:, at] = mm3((cell[kx:, :SUB], cell[kx:, SUB:]), w, NN)
         return carry
 
     chunks = nvis // wide
@@ -255,42 +255,53 @@
             src_ref=z.at[others], dst_ref=got.at[others], send_sem=sent, recv_sem=came,
             device_id=me, device_id_type=LOGICAL,
         )
-        every.wait()
-
-    with jax.named_scope("k_g"):
-        g_re, g_im = (
+        every.wait_recv()
+
+    with jax.named_scope("k_swap"):
+        sums = split(
             jnp.concatenate(
-                swap_blocks([got[v * nx : (v + 1) * nx, c, :] for v in range(ny)], rq)
+                [
+                    part
+                    for c in range(2)
+                    for part in swap_blocks(
+                        [got[v * nx : (v + 1) * nx, c, :] for v in range(ny)], rq
+                    )
+                ]
             )
-            for c in range(2)
-        )
-        g = split(
+        )
+    with jax.named_scope("k_h"):
+        both = mm3((ry[:, :hy], ry[:, hy:]), sums, NT)
+        h_re = both[:ky, :hx] - both[ky:, hx:]
+        h_im = both[:ky, hx:] + both[ky:, :hx]
+        h = split(
             jnp.concatenate(
-                [jnp.concatenate([g_re, -g_im], axis=1), jnp.concatenate([g_im, g_re], axis=1)],
+                [jnp.concatenate([h_re, -h_im], axis=1), jnp.concatenate([h_im, h_re], axis=1)],
                 axis=0,
             )
         )
-        g = split(mm3(g, (ry[0], ry[1]), NN))
-        g = mm3((rx[:, : 2 * hx], rx[:, 2 * hx :]), g, NN)
+    with jax.named_scope("k_g2"):
+        g = mm3(h, (rx[0], rx[1]), NN)
         high, low = split(g)
-        copy_of = lax.broadcasted_iota(jnp.int32, g.shape, 1) // ky
+        copy_of = lax.broadcasted_iota(jnp.int32, g.shape, 1) // kx
         g = jnp.where(copy_of == 1, low.astype(F32), high.astype(F32)).astype(BF)
         live = counts[...]
 
     def degrid(j, carry):
         at = pl.ds(pl.multiple_of(j * wide, wide), wide)
-        sums = mm(g, wv[:, at], NN)
-        w = wu[:, at]
+        sums = mm(g, wu[:, at], NN)
+        w = wv[:, at]
         block = (lax.broadcasted_iota(jnp.int32, (1, wide), 1) + j * wide) // VBLOCK
         alive = block < live
-        re = jnp.sum(sums[:kx] * w, axis=0, keepdims=True)
-        im = jnp.sum(sums[kx:] * w, axis=0, keepdims=True)
+        re = jnp.sum(sums[:ky] * w, axis=0, keepdims=True)
+        im = jnp.sum(sums[ky:] * w, axis=0, keepdims=True)
         out_ref[0, 0, :, at] = jnp.where(alive, re, 0.0)
         out_ref[1, 0, :, at] = jnp.where(alive, im, 0.0)
         return carry
 
     with jax.named_scope("l_degrid"):
         lax.fori_loop(0, nvis // wide, degrid, 0, unroll=4)
+    with jax.named_scope("m_sent"):
+        every.wait_send()
 
 
 def solution(mesh):
@@ -309,14 +320,9 @@
         base_x, re_x, im_x = compress(back_x, RANK_X)
         base_y, re_y, im_y = compress(back_y, RANK_Y)
         cell = halves(np.concatenate([base_x.T, base_y.T]), 1)
-        rx = halves(
-            np.concatenate(
-                [np.concatenate([re_x, -im_x], axis=1), np.concatenate([im_x, re_x], axis=1)]
-            ),
-            1,
-        )
-        ry = np.concatenate([re_y, im_y], axis=1).T
-        ry = halves(np.concatenate([ry, ry, ry], axis=1)[None], 0)
+        rx = np.concatenate([re_x, im_x], axis=1).T
+        rx = halves(np.concatenate([rx, rx, rx], axis=1)[None], 0)
+        ry = halves(np.concatenate([re_y, im_y]), 1)
         hx, hy = nx * rp, ny * rq
         any_spec = pl.BlockSpec(memory_space=pltpu.HBM)
         dma = pltpu.SemaphoreType.DMA
@@ -338,8 +344,8 @@
                 pltpu.VMEM((2 * hy, cols), F32),
                 pltpu.VMEM((nx * ny, 2, hy), F32),
                 pltpu.VMEM((nx * ny, 2, hy), F32),
-                pltpu.VMEM((3 * RANK_Y, nvis), BF),
-                pltpu.VMEM((RANK_X, nvis), F32),
+                pltpu.VMEM((3 * RANK_X, nvis), BF),
+                pltpu.VMEM((RANK_Y, nvis), F32),
                 dma((4,)),
                 dma((8,)),
                 dma,

time: 17.4 us -> 17.2 us (0.989)
  Pallas kernels: 16 us -> 15.8 us
    pallas_call x1, Pallas kernels: 16 us -> 15.8 us  [per_device(): pl.pallas_call(functools.partial(kernel, nx, ny, rp, rq), out_shape=pltpu...]
where the time goes in v5:
time: 17.2 us; the launch traced here: 17.1 us
  Pallas kernels  15.8 us (92%)
  between operations  0.66 us (4%)
  local copies, waits for them, and re-layouts  0.61 us (4%)
    pallas_call x1, Pallas kernels, per_device(): pl.pallas_call(functools.partial(kernel, nx, ny, rp, rq), out_shape=pltpu...  15.8 us
    unnamed x1, local copies, waits for them, and re-layouts  0.61 us

profile of v5, /device:TPU:1, one launch (start us, length us, event | category | flops | bytes accessed | tf_op | source)
XLA Modules:
  0.0 17.1 jit_solution(15141887396300498243)
XLA Ops:
  0.7 15.8 %shard_map.91 = f32[2,1,1,2048]{3,2,1,0:T(1,128)S(1)} custom-call(f32[40,1024]{1,0:T(8,128)} %constant.10.clone.tx_hbm, f32[56,256]{1,0:T(8,128)} %constant.11.clone.ty_hbm, bf16[128,512]{1,0:T(8,128)(2,1)} %constant.12.clone.cell_hbm, bf16[2,256,240]{2,1,0:T(8,128)(2,1)} %constant.13.clone.rx_hbm, bf16[96,256]{1,0:T(8,128)(2,1)} %constant.14.clone.ry_hbm, ...), custom_call_target="tpu_custom_call" | custom-call | tf_op jit(solution)/shard_map/pallas_call | solution.py:329
  16.5 0.6 %copy.11 = f32[2,1,1,2048]{3,2,1,0:T(1,128)} copy(f32[2,1,1,2048]{3,2,1,0:T(1,128)S(1)} %shard_map.91) | data formatting | bytes 32768

commit v6 on v5

--- a/solution.py
+++ b/solution.py
@@ -102,20 +102,19 @@
     return u[:, :rank], rest[:, :terms], rest[:, terms:]
 
 
-def swap_blocks(parts, size):
-    parts = list(parts)
-    width = parts[0].shape[1]
-    lane = lax.broadcasted_iota(jnp.int32, parts[0].shape, 1) // size
-    d = len(parts) // 2
-    while d:
-        low = (lane // d) % 2 == 0
-        for p in range(len(parts)):
-            if p // d % 2 == 0:
-                a, b = parts[p], parts[p + d]
-                parts[p] = jnp.where(low, a, pltpu.roll(b, size * d, 1))
-                parts[p + d] = jnp.where(low, pltpu.roll(a, width - size * d, 1), b)
-        d //= 2
-    return parts
+def pick_blocks(parts, size):
+    n = len(parts)
+    block = lax.broadcasted_iota(jnp.int32, parts[0].shape, 1) // size
+    d = 1
+    while d < n:
+        up = (block // d) % 2 == 1
+        parts = [jnp.where(up, parts[(i + d) % n], parts[i]) for i in range(n)]
+        d *= 2
+    return [parts[-s % n] for s in range(n)]
+
+
+def rolled(part, shift):
+    return part if isinstance(shift, int) and shift == 0 else pltpu.roll(part, shift, 1)
 
 
 def weights(offset, frac, shape):
@@ -199,9 +198,12 @@
         re = prod[:hx, :hy] - prod[hx:, hy:]
         im = prod[:hx, hy:] + prod[hx:, :hy]
         for c, part in enumerate((re, im)):
-            swapped = swap_blocks([part[p * nx : (p + 1) * nx] for p in range(rp)], rq)
+            swapped = pick_blocks(
+                [rolled(part[p * nx : (p + 1) * nx], p * rq) for p in range(rp)], rq
+            )
             for v in range(ny):
-                z[v * nx : (v + 1) * nx, c, :] = swapped[v]
+                turn = lax.rem(me_y + (ny - v), ny) * rq
+                z[v * nx : (v + 1) * nx, c, :] = rolled(swapped[v], turn)
 
     nvis = cells.shape[3]
     wide = WIDE
@@ -261,10 +263,10 @@
         sums = split(
             jnp.concatenate(
                 [
-                    part
+                    rolled(part, (ny - p) % ny * rq)
                     for c in range(2)
-                    for part in swap_blocks(
-                        [got[v * nx : (v + 1) * nx, c, :] for v in range(ny)], rq
+                    for p, part in enumerate(
+                        pick_blocks([got[v * nx : (v + 1) * nx, c, :] for v in range(ny)], rq)
                     )
                 ]
             )

time: 17.2 us -> 17 us (0.988)
  Pallas kernels: 15.8 us -> 15.6 us
    pallas_call x1, Pallas kernels: 15.8 us -> 15.6 us  [per_device(): pl.pallas_call(functools.partial(kernel, nx, ny, rp, rq), out_shape=pltpu...]
where the time goes in v6:
time: 17 us; the launch traced here: 16.9 us
  Pallas kernels  15.6 us (92%)
  between operations  0.66 us (4%)
  local copies, waits for them, and re-layouts  0.61 us (4%)
    pallas_call x1, Pallas kernels, per_device(): pl.pallas_call(functools.partial(kernel, nx, ny, rp, rq), out_shape=pltpu...  15.6 us
    unnamed x1, local copies, waits for them, and re-layouts  0.61 us

profile of v6, /device:TPU:1, one launch (start us, length us, event | category | flops | bytes accessed | tf_op | source)
XLA Modules:
  0.0 16.9 jit_solution(15450593888547464021)
XLA Ops:
  0.7 15.6 %shard_map.91 = f32[2,1,1,2048]{3,2,1,0:T(1,128)S(1)} custom-call(f32[40,1024]{1,0:T(8,128)} %constant.10.clone.tx_hbm, f32[56,256]{1,0:T(8,128)} %constant.11.clone.ty_hbm, bf16[128,512]{1,0:T(8,128)(2,1)} %constant.12.clone.cell_hbm, bf16[2,256,240]{2,1,0:T(8,128)(2,1)} %constant.13.clone.rx_hbm, bf16[96,256]{1,0:T(8,128)(2,1)} %constant.14.clone.ry_hbm, ...), custom_call_target="tpu_custom_call" | custom-call | tf_op jit(solution)/shard_map/pallas_call | solution.py:331
  16.3 0.6 %copy.11 = f32[2,1,1,2048]{3,2,1,0:T(1,128)} copy(f32[2,1,1,2048]{3,2,1,0:T(1,128)S(1)} %shard_map.91) | data formatting | bytes 32768

commit v7 on v6

--- a/solution.py
+++ b/solution.py
@@ -129,7 +129,7 @@
 def kernel(
     nx, ny, rp, rq, tx_hbm, ty_hbm, cell_hbm, rx_hbm, ry_hbm, f_hbm, counts_hbm, cells_hbm, fracs_hbm, out_ref,
     tx, ty, cell, rx, ry, f, counts, cells, fracs, m2, z, got, wu, wv,
-    fsem, lsem, sent, came,
+    sent, came,
 ):
     me_x = lax.axis_index("fx")
     me_y = lax.axis_index("fy")
@@ -137,73 +137,10 @@
     cols = f.shape[1]
     step = rows // 4
 
-    small = [
-        pltpu.make_async_copy(src, dst, lsem.at[i])
-        for i, (src, dst) in enumerate(
-            [
-                (tx_hbm, tx), (ty_hbm, ty), (cells_hbm, cells), (fracs_hbm, fracs),
-                (counts_hbm, counts), (cell_hbm, cell), (rx_hbm, rx), (ry_hbm, ry),
-            ]
-        )
-    ]
-    big = [
-        pltpu.make_async_copy(
-            f_hbm.at[pl.ds(i * step, step)], f.at[pl.ds(i * step, step)], fsem.at[i]
-        )
-        for i in range(4)
-    ]
-    with jax.named_scope("a_start"):
-        small[0].start()
-        big[0].start()
-        small[1].start()
-        for copy in big[1:] + small[2:]:
-            copy.start()
-
-        barrier = pltpu.get_barrier_semaphore()
-        me = me_x * ny + me_y
-        for k in SIGNALS:
-
-            @pl.when(me != k)
-            def _():
-                pl.semaphore_signal(barrier, inc=1, device_id=k, device_id_type=LOGICAL)
-
-    with jax.named_scope("b_c1"):
-        small[0].wait()
-        wx = tx[pl.ds(2 * nx + rp + me_x, 1), :]
-        phi = tx[pl.ds(2 * nx, rp), :] * wx
-        c1 = None
-        for i in range(4):
-            lanes = slice(i * step, (i + 1) * step)
-            part = jnp.concatenate(
-                [
-                    tx[c * nx : (c + 1) * nx, lanes] * phi[p : p + 1, lanes]
-                    for c in range(2)
-                    for p in range(rp)
-                ],
-                axis=0,
-            )
-            big[i].wait()
-            prod = mm3(split(part), split(f[pl.ds(i * step, step), :]), NN)
-            c1 = prod if c1 is None else c1 + prod
-
-    with jax.named_scope("c_d"):
-        small[1].wait()
-        wy = ty[pl.ds(2 * ny + rq + me_y, 1), :]
-        phi = ty[pl.ds(2 * ny, rq), :] * wy
-        for r in range(2 * ny):
-            m2[pl.ds(r * rq, rq), :] = jnp.broadcast_to(ty[pl.ds(r, 1), :], (rq, cols)) * phi
-        prod = mm3(split(c1), split(m2[...]), NT)
-        hx = nx * rp
-        hy = ny * rq
-        re = prod[:hx, :hy] - prod[hx:, hy:]
-        im = prod[:hx, hy:] + prod[hx:, :hy]
-        for c, part in enumerate((re, im)):
-            swapped = pick_blocks(
-                [rolled(part[p * nx : (p + 1) * nx], p * rq) for p in range(rp)], rq
-            )
-            for v in range(ny):
-                turn = lax.rem(me_y + (ny - v), ny) * rq
-                z[v * nx : (v + 1) * nx, c, :] = rolled(swapped[v], turn)
+    barrier = pltpu.get_barrier_semaphore()
+    me = me_x * ny + me_y
+    hx = nx * rp
+    hy = ny * rq
 
     nvis = cells.shape[3]
     wide = WIDE
@@ -227,10 +164,90 @@
 
     chunks = nvis // wide
     early = lax.div(3 - lax.rem(me_x, 4), 3) * chunks
-    with jax.named_scope("c_fill"):
-        for copy in small[2:]:
-            copy.wait()
-        lax.fori_loop(0, early, fill_v, 0)
+    def front(fsem, lsem):
+        small = [
+            pltpu.make_async_copy(src, dst, lsem.at[i])
+            for i, (src, dst) in enumerate(
+                [
+                    (tx_hbm, tx), (ty_hbm, ty), (cells_hbm, cells), (fracs_hbm, fracs),
+                    (counts_hbm, counts), (cell_hbm, cell), (rx_hbm, rx), (ry_hbm, ry),
+                ]
+            )
+        ]
+        big = [
+            pltpu.make_async_copy(
+                f_hbm.at[pl.ds(i * step, step)], f.at[pl.ds(i * step, step)], fsem.at[i]
+            )
+            for i in range(4)
+        ]
+        with jax.named_scope("a_start"):
+            small[0].start()
+            big[0].start()
+            small[1].start()
+            for copy in big[1:] + small[2:]:
+                copy.start()
+
+            for i in range(0, len(SIGNALS), 16):
+                group = SIGNALS[i : i + 16]
+
+                def tell(k):
+                    pl.semaphore_signal(barrier, inc=1, device_id=k, device_id_type=LOGICAL)
+
+                mine = functools.reduce(jnp.logical_or, [me == k for k in group])
+
+                @pl.when(jnp.logical_not(mine))
+                def _():
+                    for k in group:
+                        tell(k)
+
+                @pl.when(mine)
+                def _():
+                    for k in group:
+                        pl.when(me != k)(functools.partial(tell, k))
+
+
+        with jax.named_scope("b_c1"):
+            small[0].wait()
+            wx = tx[pl.ds(2 * nx + rp + me_x, 1), :]
+            phi = tx[pl.ds(2 * nx, rp), :] * wx
+            c1 = None
+            for i in range(4):
+                lanes = slice(i * step, (i + 1) * step)
+                part = jnp.concatenate(
+                    [
+                        tx[c * nx : (c + 1) * nx, lanes] * phi[p : p + 1, lanes]
+                        for c in range(2)
+                        for p in range(rp)
+                    ],
+                    axis=0,
+                )
+                big[i].wait()
+                prod = mm3(split(part), split(f[pl.ds(i * step, step), :]), NN)
+                c1 = prod if c1 is None else c1 + prod
+
+        with jax.named_scope("c_d"):
+            small[1].wait()
+            wy = ty[pl.ds(2 * ny + rq + me_y, 1), :]
+            phi = ty[pl.ds(2 * ny, rq), :] * wy
+            for r in range(2 * ny):
+                m2[pl.ds(r * rq, rq), :] = jnp.broadcast_to(ty[pl.ds(r, 1), :], (rq, cols)) * phi
+            prod = mm3(split(c1), split(m2[...]), NT)
+            re = prod[:hx, :hy] - prod[hx:, hy:]
+            im = prod[:hx, hy:] + prod[hx:, :hy]
+            for c, part in enumerate((re, im)):
+                swapped = pick_blocks(
+                    [rolled(part[p * nx : (p + 1) * nx], p * rq) for p in range(rp)], rq
+                )
+                for v in range(ny):
+                    turn = lax.rem(me_y + (ny - v), ny) * rq
+                    z[v * nx : (v + 1) * nx, c, :] = rolled(swapped[v], turn)
+
+        with jax.named_scope("c_fill"):
+            for copy in small[2:]:
+                copy.wait()
+            lax.fori_loop(0, early, fill_v, 0)
+
+    pl.run_scoped(front, pltpu.SemaphoreType.DMA((4,)), pltpu.SemaphoreType.DMA((8,)))
 
     with jax.named_scope("d_barrier"):
         pl.semaphore_wait(barrier, nx * ny - 1)
@@ -348,8 +365,6 @@
                 pltpu.VMEM((nx * ny, 2, hy), F32),
                 pltpu.VMEM((3 * RANK_X, nvis), BF),
                 pltpu.VMEM((RANK_Y, nvis), F32),
-                dma((4,)),
-                dma((8,)),
                 dma,
                 dma,
             ],

time: 17 us -> 16.9 us (level)
  no operation moved by 1% of the time
where the time goes in v7:
time: 16.9 us; the launch traced here: 16.8 us
  Pallas kernels  15.5 us (92%)
  between operations  0.66 us (4%)
  local copies, waits for them, and re-layouts  0.61 us (4%)
    pallas_call x1, Pallas kernels, per_device(): pl.pallas_call(functools.partial(kernel, nx, ny, rp, rq), out_shape=pltpu...  15.5 us
    unnamed x1, local copies, waits for them, and re-layouts  0.61 us

profile of v7, /device:TPU:1, one launch (start us, length us, event | category | flops | bytes accessed | tf_op | source)
XLA Modules:
  0.0 16.8 jit_solution(13811059333223453980)
XLA Ops:
  0.7 15.5 %shard_map.91 = f32[2,1,1,2048]{3,2,1,0:T(1,128)S(1)} custom-call(f32[40,1024]{1,0:T(8,128)} %constant.10.clone.tx_hbm, f32[56,256]{1,0:T(8,128)} %constant.11.clone.ty_hbm, bf16[128,512]{1,0:T(8,128)(2,1)} %constant.12.clone.cell_hbm, bf16[2,256,240]{2,1,0:T(8,128)(2,1)} %constant.13.clone.rx_hbm, bf16[96,256]{1,0:T(8,128)(2,1)} %constant.14.clone.ry_hbm, ...), custom_call_target="tpu_custom_call" | custom-call | tf_op jit(solution)/shard_map/pallas_call | solution.py:348
  16.2 0.6 %copy.11 = f32[2,1,1,2048]{3,2,1,0:T(1,128)} copy(f32[2,1,1,2048]{3,2,1,0:T(1,128)S(1)} %shard_map.91) | data formatting | bytes 32768

commit v8 on v7

--- a/solution.py
+++ b/solution.py
@@ -187,24 +187,11 @@
             for copy in big[1:] + small[2:]:
                 copy.start()
 
-            for i in range(0, len(SIGNALS), 16):
-                group = SIGNALS[i : i + 16]
-
-                def tell(k):
+            for k in SIGNALS:
+
+                @pl.when(me != k)
+                def _():
                     pl.semaphore_signal(barrier, inc=1, device_id=k, device_id_type=LOGICAL)
-
-                mine = functools.reduce(jnp.logical_or, [me == k for k in group])
-
-                @pl.when(jnp.logical_not(mine))
-                def _():
-                    for k in group:
-                        tell(k)
-
-                @pl.when(mine)
-                def _():
-                    for k in group:
-                        pl.when(me != k)(functools.partial(tell, k))
-
 
         with jax.named_scope("b_c1"):
             small[0].wait()

time: 16.9 us -> 16.9 us (level)
  no operation moved by 1% of the time
where the time goes in v8:
time: 16.9 us; the launch traced here: 16.8 us
  Pallas kernels  15.5 us (92%)
  between operations  0.66 us (4%)
  local copies, waits for them, and re-layouts  0.61 us (4%)
    pallas_call x1, Pallas kernels, per_device(): pl.pallas_call(functools.partial(kernel, nx, ny, rp, rq), out_shape=pltpu...  15.5 us
    unnamed x1, local copies, waits for them, and re-layouts  0.61 us

profile of v8, /device:TPU:1, one launch (start us, length us, event | category | flops | bytes accessed | tf_op | source)
XLA Modules:
  0.0 16.8 jit_solution(8208495826060377947)
XLA Ops:
  0.7 15.5 %shard_map.91 = f32[2,1,1,2048]{3,2,1,0:T(1,128)S(1)} custom-call(f32[40,1024]{1,0:T(8,128)} %constant.10.clone.tx_hbm, f32[56,256]{1,0:T(8,128)} %constant.11.clone.ty_hbm, bf16[128,512]{1,0:T(8,128)(2,1)} %constant.12.clone.cell_hbm, bf16[2,256,240]{2,1,0:T(8,128)(2,1)} %constant.13.clone.rx_hbm, bf16[96,256]{1,0:T(8,128)(2,1)} %constant.14.clone.ry_hbm, ...), custom_call_target="tpu_custom_call" | custom-call | tf_op jit(solution)/shard_map/pallas_call | solution.py:335
  16.2 0.6 %copy.11 = f32[2,1,1,2048]{3,2,1,0:T(1,128)} copy(f32[2,1,1,2048]{3,2,1,0:T(1,128)S(1)} %shard_map.91) | data formatting | bytes 32768
